TPU v7x, 32 devices: a whole 2x2x4 slice. The times are simulated.
32 devices in a mesh: dp: 8 (over y, x, core), mp: 4 (over z).
Axes of the slice: x: 2, y: 2, z: 4, core: 2. Of those that a mesh axis runs over, the one named last changes fastest.
Arguments:
- tokens: bfloat16 [20480, 1024], P(('dp', 'mp')), may hold values from -6 to 6
- context: int32 [40], P('dp'), may hold values from 0 to 475, as said below
- timestep: int32 [40], P('dp'), may hold values from 1 to 5000
- time_weight: float32 [1024], replicated, may hold values from -6 to 6
- time_bias: float32 [1024], replicated, may hold values from -3 to 3
- qkv_weight: bfloat16 [3, 1024, 1024], P(None, 'dp', 'mp'), may hold values from -0.1875 to 0.1875
- qv_bias: bfloat16 [16, 128], P('mp', 'dp'), may hold values from -3 to 3
- out_weight: bfloat16 [1024, 1024], P('mp', 'dp'), may hold values from -1 to 1
- out_bias: float32 [1024], replicated, may hold values from -3 to 3
- gain_one: float32 [1024], replicated, may hold values from 0.5 to 1.5
- shift_one: float32 [1024], replicated, may hold values from -3 to 3
- up_weight: bfloat16 [4096, 1024], P('mp', 'dp'), may hold values from -0.1875 to 0.1875
- up_bias: bfloat16 [32, 128], P('mp', 'dp'), may hold values from -3 to 3
- down_weight: bfloat16 [4096, 1024], P('mp', 'dp'), may hold values from -0.09375 to 0.09375
- down_bias: float32 [1024], replicated, may hold values from -3 to 3
- gain_two: float32 [1024], replicated, may hold values from 0.5 to 1.5
- shift_two: float32 [1024], replicated, may hold values from -3 to 3
- cotangent: bfloat16 [20480, 1024], P(('dp', 'mp')), may hold values from -6 to 6
Outputs:
- layer_out: bfloat16 [20480, 1024], P(('dp', 'mp'))
- grad_tokens: float32 [20480, 1024], P(('dp', 'mp'))
- grad_time_weight: float32 [1024], P(('dp', 'mp'))
- grad_time_bias: float32 [1024], P(('dp', 'mp'))
- grad_qkv_weight: float32 [3, 1024, 1024], P(None, 'dp', 'mp')
- grad_qv_bias: float32 [16, 128], P('mp', 'dp')
- grad_out_weight: float32 [1024, 1024], P('mp', 'dp')
- grad_out_bias: float32 [1024], P(('dp', 'mp'))
- grad_gain_one: float32 [1024], P(('dp', 'mp'))
- grad_shift_one: float32 [1024], P(('dp', 'mp'))
- grad_up_weight: float32 [4096, 1024], P('mp', 'dp')
- grad_up_bias: float32 [32, 128], P('mp', 'dp')
- grad_down_weight: float32 [4096, 1024], P('mp', 'dp')
- grad_down_bias: float32 [1024], P(('dp', 'mp'))
- grad_gain_two: float32 [1024], P(('dp', 'mp'))
- grad_shift_two: float32 [1024], P(('dp', 'mp'))
Inputs may be any that keep to these rules, and one draw needn't show every extreme that they name: Sequence b holds context[b] context tokens followed by 25 block tokens; its remaining positions are padding and are never attended to.
All inputs are finite; a program needn't handle non-finite values.
Results may differ from a plain program's by a relative error of at most 0.019.
Values may be sent and summed in bfloat16 or wider, within the bound.
A program may use at most 128 MiB of HBM per device.

v0:
```python
import math

import jax
import jax.numpy as jnp
from jax import lax
from jax.sharding import PartitionSpec as P

BLOCK = 25
TSTEPS = 5000


LN_EPS = 1e-05
MASKED = -1e30


def layer_norm(values_in, gain, shift):
    average = jnp.mean(values_in, axis=-1, keepdims=True)
    centred = values_in - average
    variance = jnp.mean(centred * centred, axis=-1, keepdims=True)
    return centred * lax.rsqrt(variance + LN_EPS) * gain + shift


def gelu_exact(values_in):
    return jax.nn.gelu(values_in, approximate=False)


def times_rows(left, right):
    return lax.dot_general(
        left, right, (((1,), (1,)), ((), ())), preferred_element_type=jnp.float32
    )


def times_cols(left, right):
    return lax.dot_general(
        left, right, (((0,), (0,)), ((), ())), preferred_element_type=jnp.float32
    )


def key_scores(queries, key_rows, live_len):
    head_size = queries.shape[-1]
    scores = jnp.einsum("qhd,khd->hqk", queries, key_rows, preferred_element_type=jnp.float32)
    scores = scores * (1.0 / math.sqrt(head_size))
    usable = jnp.arange(key_rows.shape[0]) < live_len
    return jnp.where(usable[None, None, :], scores, MASKED)


def forward_keys(key_count, record):
    seq_block, live_len = record
    queries = seq_block[:, 0]
    key_rows = seq_block[:key_count, 1]
    values = seq_block[:key_count, 2]
    scores = key_scores(queries, key_rows, live_len)
    row_max = jnp.max(scores, axis=-1, keepdims=True)
    expo_vals = jnp.exp(scores - row_max)
    total_e = jnp.sum(expo_vals, axis=-1, keepdims=True)
    prob_low = (expo_vals / total_e).astype(jnp.bfloat16)
    mixed_out = jnp.einsum("hqk,khd->qhd", prob_low, values, preferred_element_type=jnp.float32)
    return (mixed_out.astype(jnp.bfloat16), (row_max + jnp.log(total_e))[..., 0])


def backward_keys(key_count, record):
    seq_block, live_len, log_total, grad_out = record
    queries = seq_block[:, 0]
    key_rows = seq_block[:key_count, 1]
    values = seq_block[:key_count, 2]
    scale_factor = 1.0 / math.sqrt(queries.shape[-1])
    scores = key_scores(queries, key_rows, live_len)
    probs = jnp.exp(scores - log_total[..., None])
    grad_v = jnp.einsum(
        "hqk,qhd->khd", probs.astype(jnp.bfloat16), grad_out, preferred_element_type=jnp.float32
    )
    grad_p = jnp.einsum("qhd,khd->hqk", grad_out, values, preferred_element_type=jnp.float32)
    inner = jnp.sum(probs * grad_p, axis=-1, keepdims=True)
    grad_s = (probs * (grad_p - inner)).astype(jnp.bfloat16)
    grad_q = (
        jnp.einsum("hqk,khd->qhd", grad_s, key_rows, preferred_element_type=jnp.float32)
        * scale_factor
    )
    grad_k = (
        jnp.einsum("hqk,qhd->khd", grad_s, queries, preferred_element_type=jnp.float32)
        * scale_factor
    )
    return jnp.stack(
        [grad_q.astype(jnp.bfloat16), grad_k.astype(jnp.bfloat16), grad_v.astype(jnp.bfloat16)],
        axis=1,
    )


def body(
    tokens,
    context,
    timestep,
    time_weight,
    time_bias,
    qkv_weight,
    qv_bias,
    out_weight,
    out_bias,
    gain_one,
    shift_one,
    up_weight,
    up_bias,
    down_weight,
    down_bias,
    gain_two,
    shift_two,
    cotangent,
):
    mp_count = lax.axis_size("mp")
    mp_index = lax.axis_index("mp")
    shard_rows = tokens.shape[0]
    seq_count = context.shape[0]
    total_rows = shard_rows * mp_count
    seq_len = total_rows // seq_count
    qkv_weight, out_weight, qv_bias, up_weight, down_weight, up_bias = (
        lax.all_gather(qkv_weight, "dp", axis=1, tiled=True),
        lax.all_gather(out_weight, "dp", axis=1, tiled=True),
        lax.all_gather(qv_bias, "dp", axis=1, tiled=True),
        lax.all_gather(up_weight, "dp", axis=1, tiled=True),
        lax.all_gather(down_weight, "dp", axis=1, tiled=True),
        lax.all_gather(up_bias, "dp", axis=1, tiled=True),
    )
    local_width = qkv_weight.shape[2]
    local_heads = qv_bias.shape[0]
    head_size = qv_bias.shape[1] // 2
    row_ids = mp_index * shard_rows + jnp.arange(shard_rows, dtype=jnp.int32)
    owner = (row_ids // seq_len)[:, None] == jnp.arange(seq_count, dtype=jnp.int32)[None, :]
    frac_table = timestep.astype(jnp.float32) / TSTEPS
    fraction = jnp.sum(jnp.where(owner, frac_table[None, :], 0.0), axis=1)
    h_zero = tokens.astype(jnp.float32) + fraction[:, None] * time_weight + time_bias
    h_low = h_zero.astype(jnp.bfloat16)
    h_all = lax.all_gather(h_low, "mp", axis=0, tiled=True)
    bias_f = qv_bias.astype(jnp.float32)
    qkv_bias = jnp.stack(
        [
            bias_f[:, :head_size].reshape(local_width),
            jnp.zeros((local_width,), jnp.float32),
            bias_f[:, head_size:].reshape(local_width),
        ]
    )
    qkv_rows = (
        jnp.einsum("td,cde->tce", h_all, qkv_weight, preferred_element_type=jnp.float32) + qkv_bias
    ).astype(jnp.bfloat16)
    live_all = context + BLOCK
    seq_qkv = qkv_rows.reshape(seq_count, seq_len, 3, local_heads, head_size)
    mixed_seq, log_totals = lax.map(
        lambda record: forward_keys(seq_len, record), (seq_qkv, live_all)
    )
    attn_flat = mixed_seq.reshape(total_rows, local_width)
    branch_a = (
        lax.psum_scatter(
            jnp.dot(attn_flat, out_weight, preferred_element_type=jnp.float32),
            "mp",
            scatter_dimension=0,
            tiled=True,
        )
        + out_bias
    )
    y_one, ln_one_back = jax.vjp(layer_norm, h_zero + branch_a, gain_one, shift_one)
    y_low = y_one.astype(jnp.bfloat16)
    y_all = lax.all_gather(y_low, "mp", axis=0, tiled=True)
    pre_act = times_rows(y_all, up_weight) + up_bias.reshape(-1).astype(jnp.float32)
    hidden, gelu_back = jax.vjp(gelu_exact, pre_act)
    hidden_low = hidden.astype(jnp.bfloat16)
    branch_f = (
        lax.psum_scatter(
            jnp.dot(hidden_low, down_weight, preferred_element_type=jnp.float32).astype(
                jnp.bfloat16
            ),
            "mp",
            scatter_dimension=0,
            tiled=True,
        ).astype(jnp.float32)
        + down_bias
    )
    y_two, ln_two_back = jax.vjp(layer_norm, y_one + branch_f, gain_two, shift_two)
    layer_out = y_two.astype(jnp.bfloat16)
    grad_z2, grad_gain_two, grad_shift_two = ln_two_back(cotangent.astype(jnp.float32))
    grad_f_low = grad_z2.astype(jnp.bfloat16)
    grad_down_bias = jnp.sum(grad_f_low.astype(jnp.float32), axis=0)
    grad_f_all = lax.all_gather(grad_f_low, "mp", axis=0, tiled=True)
    (grad_pre,) = gelu_back(times_rows(grad_f_all, down_weight))
    grad_pre_low = grad_pre.astype(jnp.bfloat16)
    grad_up_weight = times_cols(grad_pre_low, y_all)
    grad_down_weight = times_cols(hidden_low, grad_f_all)
    grad_up_bias = jnp.sum(grad_pre_low.astype(jnp.float32), axis=0).reshape(up_bias.shape)
    grad_y1 = grad_z2 + lax.psum_scatter(
        jnp.dot(grad_pre_low, up_weight, preferred_element_type=jnp.float32).astype(jnp.bfloat16),
        "mp",
        scatter_dimension=0,
        tiled=True,
    ).astype(jnp.float32)
    grad_z1, grad_gain_one, grad_shift_one = ln_one_back(grad_y1)
    grad_a_low = grad_z1.astype(jnp.bfloat16)
    grad_out_bias = jnp.sum(grad_a_low.astype(jnp.float32), axis=0)
    grad_a_all = lax.all_gather(grad_a_low, "mp", axis=0, tiled=True)
    grad_attn = times_rows(grad_a_all, out_weight).astype(jnp.bfloat16)
    grad_out_weight = times_cols(attn_flat, grad_a_all)
    grad_seq = lax.map(
        lambda record: backward_keys(seq_len, record),
        (
            seq_qkv,
            live_all,
            log_totals,
            grad_attn.reshape(seq_count, seq_len, local_heads, head_size),
        ),
    )
    grad_qkv = grad_seq.reshape(total_rows, 3, local_width)
    grad_qkv_weight = jnp.einsum("td,tce->cde", h_all, grad_qkv, preferred_element_type=jnp.float32)
    bias_sums = jnp.sum(grad_qkv.astype(jnp.float32), axis=0)
    grad_qv_bias = jnp.concatenate(
        [
            bias_sums[0].reshape(local_heads, head_size),
            bias_sums[2].reshape(local_heads, head_size),
        ],
        axis=1,
    )
    grad_tokens = grad_z1 + lax.psum_scatter(
        jnp.einsum("tce,cde->td", grad_qkv, qkv_weight, preferred_element_type=jnp.float32).astype(
            jnp.bfloat16
        ),
        "mp",
        scatter_dimension=0,
        tiled=True,
    ).astype(jnp.float32)
    grad_time_weight = jnp.sum(fraction[:, None] * grad_tokens, axis=0)
    grad_time_bias = jnp.sum(grad_tokens, axis=0)
    (
        grad_qkv_weight,
        grad_out_weight,
        grad_qv_bias,
        grad_up_weight,
        grad_down_weight,
        grad_up_bias,
    ) = (
        lax.psum_scatter(grad_qkv_weight, "dp", scatter_dimension=1, tiled=True),
        lax.psum_scatter(grad_out_weight, "dp", scatter_dimension=1, tiled=True),
        lax.psum_scatter(grad_qv_bias, "dp", scatter_dimension=1, tiled=True),
        lax.psum_scatter(grad_up_weight, "dp", scatter_dimension=1, tiled=True),
        lax.psum_scatter(grad_down_weight, "dp", scatter_dimension=1, tiled=True),
        lax.psum_scatter(grad_up_bias, "dp", scatter_dimension=1, tiled=True),
    )
    (
        grad_out_bias,
        grad_gain_one,
        grad_shift_one,
        grad_gain_two,
        grad_shift_two,
        grad_down_bias,
        grad_time_weight,
        grad_time_bias,
    ) = (
        lax.psum_scatter(grad_out_bias, ("dp", "mp"), scatter_dimension=0, tiled=True),
        lax.psum_scatter(grad_gain_one, ("dp", "mp"), scatter_dimension=0, tiled=True),
        lax.psum_scatter(grad_shift_one, ("dp", "mp"), scatter_dimension=0, tiled=True),
        lax.psum_scatter(grad_gain_two, ("dp", "mp"), scatter_dimension=0, tiled=True),
        lax.psum_scatter(grad_shift_two, ("dp", "mp"), scatter_dimension=0, tiled=True),
        lax.psum_scatter(grad_down_bias, ("dp", "mp"), scatter_dimension=0, tiled=True),
        lax.psum_scatter(grad_time_weight, ("dp", "mp"), scatter_dimension=0, tiled=True),
        lax.psum_scatter(grad_time_bias, ("dp", "mp"), scatter_dimension=0, tiled=True),
    )
    return (
        layer_out,
        grad_tokens,
        grad_time_weight,
        grad_time_bias,
        grad_qkv_weight,
        grad_qv_bias,
        grad_out_weight,
        grad_out_bias,
        grad_gain_one,
        grad_shift_one,
        grad_up_weight,
        grad_up_bias,
        grad_down_weight,
        grad_down_bias,
        grad_gain_two,
        grad_shift_two,
    )


def solution(mesh):
    placed = (
        P(("dp", "mp"), None),
        P("dp"),
        P("dp"),
        P(),
        P(),
        P(None, "dp", "mp"),
        P("mp", "dp"),
        P("mp", "dp"),
        P(),
        P(),
        P(),
        P("mp", "dp"),
        P("mp", "dp"),
        P("mp", "dp"),
        P(),
        P(),
        P(),
        P(("dp", "mp"), None),
    )
    return jax.shard_map(
        body,
        mesh=mesh,
        in_specs=placed,
        out_specs=(
            P(("dp", "mp"), None),
            P(("dp", "mp"), None),
            P(("dp", "mp")),
            P(("dp", "mp")),
            P(None, "dp", "mp"),
            P("mp", "dp"),
            P("mp", "dp"),
            P(("dp", "mp")),
            P(("dp", "mp")),
            P(("dp", "mp")),
            P("mp", "dp"),
            P("mp", "dp"),
            P("mp", "dp"),
            P(("dp", "mp")),
            P(("dp", "mp")),
            P(("dp", "mp")),
        ),
        check_vma=False,
    )
```

profile of v0, /device:TPU:0, one launch (start us, length us, event | category | flops | bytes accessed | tf_op | source)
XLA Modules:
  0.0 1414.3 jit_solution(10360146816921266265)
XLA Ops:
  8.8 2.8 fusion.47
  11.7 10.6 all-gather
  22.7 9.8 all_gather.33
  32.5 5.7 all-gather.12.cloned.1.call-done
  38.2 100.2 %all-gather.10.cloned.1.call-done = bf16[2560,1024]{1,0:T(8,128)(2,1)} async-done(((bf16[640,1024]{1,0:T(8,128)(2,1)}), bf16[2560,1024]{1,0:T(8,128)(2,1)}) %all-gather.10.cloned.1.call-update) | async-done | bytes 5242896 | tf_op jit(solution)/shard_map/all_gather | solution.py:132
  138.4 9.2 add_convert_fusion.1
  147.6 12.2 reshape.203
  159.9 12.0 copy.94
  171.9 31.1 %while.22 = (s32[]{:T(128)}, bf16[5,512,4,64]{1,3,2,0:T(8,128)(2,1)S(1)}, f32[5,4,512]{2,1,0:T(4,128)}, bf16[5,512,3,4,64]{1,4,3,2,0:T(8,128)(2,1)}, s32[5]{0:T(128)S(1)}, /*index=5*/s32[]{:T(128)}) while((s32[]{:T(128)}, bf16[5,512,4,64]{1,3,2,0:T(8,128)(2,1)S(1)}, f32[5,4,512]{2,1,0:T(4,128)}, bf16[5,512,3,4,64]{1,4,3,2,0:T(8,128)(2,1)}, ...), condition=%wide.region_4.5_spmd, body=%wide.region_1.4_spmd.sunk | while | flops 281147904 | bytes 15272541 | solution.py:146
  205.5 5.6 fusion.65
  212.2 175.4 %reduce-scatter.15.cloned.1.call-done = f32[640,1024]{1,0:T(8,128)} async-done(((f32[2560,1024]{1,0:T(8,128)}), f32[640,1024]{1,0:T(8,128)}) %reduce-scatter.15.cloned.1.call-update) | async-done | bytes 2621456 | tf_op jit(solution)/shard_map/reduce_scatter | solution.py:151
  387.7 2.9 fusion.63
  391.0 1.5 fusion.48
  393.2 8.9 all-gather.1
  402.2 16.4 %all-gather.16.cloned.1.call-done = bf16[1024,1024]{1,0:T(8,128)(2,1)} async-done(((bf16[1024,128]{1,0:T(8,128)(2,1)}), bf16[1024,1024]{1,0:T(8,128)(2,1)}) %all-gather.16.cloned.1.call-update) | async-done | bytes 2097168 | tf_op jit(solution)/shard_map/all_gather | solution.py:119
  418.6 100.1 %all-gather.14.cloned.1.call-done = bf16[2560,1024]{1,0:T(8,128)(2,1)} async-done(((bf16[640,1024]{1,0:T(8,128)(2,1)}), bf16[2560,1024]{1,0:T(8,128)(2,1)}) %all-gather.14.cloned.1.call-update) | async-done | bytes 5242896 | tf_op jit(solution)/shard_map/all_gather | solution.py:161
  518.6 32.1 %multiply_convert_fusion.1 = (bf16[2560,1024]{1,0:T(8,128)(2,1)}, f32[2560,1024]{1,0:T(8,128)}, f32[2560,1024]{1,0:T(8,128)}) fusion(f32[1024]{0:T(1024)S(1)} %bitcast.187, bf16[2560,1024]{1,0:T(8,128)(2,1)} %all-gather.14.cloned.1.call-done, bf16[1024,1024]{1,0:T(8,128)(2,1)} %all-gather.16.cloned.1.call-done), kind=kOutput, calls=%fused_computation.55 | convolution fusion | flops 5541724160 | bytes 33558528 | tf_op jit(solution)/shard_map/dot_general | solution.py:28
  550.8 10.2 convolution_convert_fusion.1
  561.3 92.0 %reduce-scatter.17.cloned.1.call-done = bf16[640,1024]{1,0:T(8,128)(2,1)} async-done(((bf16[2560,1024]{1,0:T(8,128)(2,1)}), bf16[640,1024]{1,0:T(8,128)(2,1)}) %reduce-scatter.17.cloned.1.call-update) | async-done | bytes 1310736 | tf_op jit(solution)/shard_map/reduce_scatter | solution.py:166
  653.3 2.3 fusion.61
  656.1 1.5 fusion.46
  657.6 2.1 fusion.60
  659.8 1.5 copy-done
  661.3 1.9 convert_reduce_fusion.3
  663.3 98.6 %all-gather.20.cloned.1.call-done = bf16[2560,1024]{1,0:T(8,128)(2,1)} async-done(((bf16[640,1024]{1,0:T(8,128)(2,1)}), bf16[2560,1024]{1,0:T(8,128)(2,1)}) %all-gather.20.cloned.1.call-update) | async-done | bytes 5242896 | tf_op jit(solution)/shard_map/all_gather | solution.py:181
  761.9 16.5 %convert_reduce_fusion = (f32[1024]{0:T(1024)S(1)}, bf16[2560,1024]{1,0:T(8,128)(2,1)S(1)}) fusion(f32[2560,1024]{1,0:T(8,128)} %get-tuple-element.266, f32[2560,1024]{1,0:T(8,128)} %get-tuple-element.278, f32[1024]{0:T(1024)S(1)} %bitcast.188, bf16[2560,1024]{1,0:T(8,128)(2,1)} %all-gather.20.cloned.1.call-done, ...), kind=kOutput, calls=%fused_computation.53 | convolution fusion | flops 5413272576 | bytes 33562624 | tf_op jit(solution)/shard_map/dot_general | solution.py:28
  778.5 2.4 copy-done.27
  780.9 7.3 convolution_convert_fusion
  788.2 92.2 %reduce-scatter.19.cloned.1.call-done = bf16[640,1024]{1,0:T(8,128)(2,1)} async-done(((bf16[2560,1024]{1,0:T(8,128)(2,1)}), bf16[640,1024]{1,0:T(8,128)(2,1)}) %reduce-scatter.19.cloned.1.call-update) | async-done | bytes 1310736 | tf_op jit(solution)/shard_map/reduce_scatter | solution.py:187
  880.5 3.5 multiply_reduce_fusion.1
  885.2 1.5 copy-done.2
  888.9 97.8 %all-gather.22.cloned.1.call-done = bf16[2560,1024]{1,0:T(8,128)(2,1)} async-done(((bf16[640,1024]{1,0:T(8,128)(2,1)}), bf16[2560,1024]{1,0:T(8,128)(2,1)}) %all-gather.22.cloned.1.call-update) | async-done | bytes 5242896 | tf_op jit(solution)/shard_map/all_gather | solution.py:196
  986.7 5.1 convolution_convert_fusion.2
  991.8 4.2 reshape.198
  996.1 3.0 copy.99
  999.1 60.0 %while.23 = (s32[]{:T(128)}, bf16[5,512,3,4,64]{1,4,3,2,0:T(8,128)(2,1)}, bf16[5,512,3,4,64]{1,4,3,2,0:T(8,128)(2,1)}, s32[5]{0:T(128)S(1)}, f32[5,4,512]{2,1,0:...) while((s32[]{:T(128)}, bf16[5,512,3,4,64]{1,4,3,2,0:T(8,128)(2,1)}, ...), condition=%wide.region_18.19_spmd, body=%wide.region_16.18_spmd.sunk | while | flops 689830400 | bytes 37285476 | solution.py:199
  1003.0 2.4 multiply_reduce_fusion.7
  1005.4 1.4 multiply_convert_fusion.3
  1008.0 2.1 fusion.113
  1015.0 2.4 multiply_reduce_fusion.7
  1017.4 1.4 multiply_convert_fusion.3
  1020.0 2.1 fusion.113
  1027.0 2.4 multiply_reduce_fusion.7
  1032.0 2.1 fusion.113
  1039.0 2.4 multiply_reduce_fusion.7
  1044.0 2.1 fusion.113
  1051.0 2.4 multiply_reduce_fusion.7
  1056.0 2.1 fusion.113
  1059.1 2.7 convert_reduce_fusion.1
  1061.9 7.7 copy.100
  1070.3 9.7 reshape.187
  1080.3 9.7 fusion.49
  1090.0 8.3 bitcast_convert_fusion
  1098.4 10.5 fusion.68
  1108.9 10.5 fusion.67
  1119.5 5.9 fusion.66
  1128.2 33.3 %reduce-scatter.23.cloned.1.call-done = f32[3,128,256]{1,2,0:T(8,128)} async-done(((f32[3,1024,256]{1,2,0:T(8,128)}), f32[3,128,256]{1,2,0:T(8,128)}) %reduce-scatter.23.cloned.1.call-update) | async-done | bytes 393232 | tf_op jit(solution)/shard_map/reduce_scatter | solution.py:236
  1161.5 1.9 copy.102
  1163.4 94.1 %reduce-scatter.21.cloned.1.call-done = bf16[640,1024]{1,0:T(8,128)(2,1)} async-done(((bf16[2560,1024]{1,0:T(8,128)(2,1)}), bf16[640,1024]{1,0:T(8,128)(2,1)}) %reduce-scatter.21.cloned.1.call-update) | async-done | bytes 1310736 | tf_op jit(solution)/shard_map/reduce_scatter | solution.py:218
  1257.5 3.4 fusion.58
  1260.9 41.5 %all-reduce.8 = (f32[1024]{0:T(1024)S(1)}, f32[1024]{0:T(1024)S(1)}, f32[1024]{0:T(1024)S(1)}, f32[1024]{0:T(1024)S(1)}, f32[1024]{0:T(1024)S(1)}, /*index=5*/f3...) all-reduce(f32[1024]{0:T(1024)S(1)} %get-tuple-element.220, ...), channel_id=6, replica_groups=mesh['dp'=8,'mp'=4] {'dp','mp'}, use_global_device_ids=true, to_apply=%region_21.22.clone | all-reduce | flops 8192 | bytes 65536
  1307.1 6.0 reduce-scatter.29.cloned.1.call-done
  1313.1 54.8 %reduce-scatter.27.cloned.1.call-done = f32[1024,128]{1,0:T(8,128)} async-done(((f32[1024,1024]{1,0:T(8,128)}), f32[1024,128]{1,0:T(8,128)}) %reduce-scatter.27.cloned.1.call-update) | async-done | bytes 524304 | tf_op jit(solution)/shard_map/reduce_scatter | solution.py:239
  1367.9 39.6 %reduce-scatter.25.cloned.1.call-done = f32[256,128]{1,0:T(8,128)} async-done(((f32[256,1024]{1,0:T(8,128)}), f32[256,128]{1,0:T(8,128)}) %reduce-scatter.25.cloned.1.call-update) | async-done | bytes 131088 | tf_op jit(solution)/shard_map/reduce_scatter | solution.py:237
  (212 shorter events, 85.1 us)
Async XLA Ops:
  7.2 15.5 %copy-start.7 = (bf16[256,128]{1,0:T(8,128)(2,1)S(1)}, bf16[256,128]{1,0:T(8,128)(2,1)}, u32[]{:S(2)}) copy-start(bf16[256,128]{1,0:T(8,128)(2,1)} %param.29) | copy-start | bytes 196612
  7.2 25.3 %copy-start.24 = (s32[5]{0:T(128)S(1)}, s32[5]{0:T(128)}, u32[]{:S(2)}) copy-start(s32[5]{0:T(128)} %param.23) | copy-start | bytes 64
  7.2 31.0 %all-gather.12.cloned.1.call-start = ((), (), s32[]{:S(2)}) async-start(), calls=%async_computation.11 | async-start | bytes 1769472 | tf_op jit(solution)/shard_map/all_gather | solution.py:116
  7.9 130.5 %all-gather.10.cloned.1.call-start = ((), (), s32[]{:S(2)}) async-start(), calls=%async_computation.10 | async-start | bytes 6553600 | tf_op jit(solution)/shard_map/all_gather | solution.py:132
  8.7 378.9 %copy-start.8 = (f32[640]{0:T(1024)}, f32[640]{0:T(1024)S(1)}, u32[]{:S(2)}) copy-start(f32[640]{0:T(1024)S(1)} %select_reduce_fusion) | copy-start | bytes 7684
  11.6 376.0 %reduce-scatter.15.cloned.1.call-start = ((), (), s32[]{:S(2)}) async-start(), calls=%async_computation.12 | async-start | bytes 13107200 | tf_op jit(solution)/shard_map/reduce_scatter | solution.py:151
  203.0 8.0 copy-start.25
  204.5 1.1 copy-start.4
  211.1 176.6 %copy-start.11 = (f32[1024]{0:T(1024)S(1)}, f32[1024]{0:T(1024)}, u32[]{:S(2)}) copy-start(f32[1024]{0:T(1024)} %param.26) | copy-start | bytes 12292
  211.1 176.6 %copy-start.12 = (f32[1024]{0:T(1024)S(1)}, f32[1024]{0:T(1024)}, u32[]{:S(2)}) copy-start(f32[1024]{0:T(1024)} %param.25) | copy-start | bytes 12292
  211.1 176.6 %copy-start.20 = (f32[1024]{0:T(1024)S(1)}, f32[1024]{0:T(1024)}, u32[]{:S(2)}) copy-start(f32[1024]{0:T(1024)} %param.30) | copy-start | bytes 12292
  211.1 207.5 %all-gather.16.cloned.1.call-start = ((), (), s32[]{:S(2)}) async-start(), calls=%async_computation.14 | async-start | bytes 2359296 | tf_op jit(solution)/shard_map/all_gather | solution.py:119
  211.7 179.3 %copy-start.10 = (f32[1024]{0:T(1024)S(1)}, f32[1024]{0:T(1024)}, u32[]{:S(2)}) copy-start(f32[1024]{0:T(1024)} %param.31) | copy-start | bytes 12292
  211.7 179.3 %copy-start.13 = (f32[1024]{0:T(1024)S(1)}, f32[1024]{0:T(1024)}, u32[]{:S(2)}) copy-start(f32[1024]{0:T(1024)} %param.32) | copy-start | bytes 12292
  211.7 306.9 %all-gather.14.cloned.1.call-start = ((), (), s32[]{:S(2)}) async-start(), calls=%async_computation.13 | async-start | bytes 6553600 | tf_op jit(solution)/shard_map/all_gather | solution.py:161
  390.6 2.6 copy-start.21
  392.6 158.2 %all-gather.18.cloned.1.call-start = ((), (), s32[]{:S(2)}) async-start(), calls=%async_computation.15 | async-start | bytes 2359296 | tf_op jit(solution)/shard_map/all_gather | solution.py:120
  393.2 260.2 %reduce-scatter.17.cloned.1.call-start = ((), (), s32[]{:S(2)}) async-start(), calls=%async_computation.16 | async-start | bytes 6553600 | tf_op jit(solution)/shard_map/reduce_scatter | solution.py:166
  561.0 92.3 %copy-start.18 = (f32[1024]{0:T(1024)S(1)}, f32[1024]{0:T(1024)}, u32[]{:S(2)}) copy-start(f32[1024]{0:T(1024)} %param.36) | copy-start | bytes 12292
  561.0 95.1 %copy-start.14 = (f32[1024]{0:T(1024)S(1)}, f32[1024]{0:T(1024)}, u32[]{:S(2)}) copy-start(f32[1024]{0:T(1024)} %param.37) | copy-start | bytes 12292
  561.1 200.9 %all-gather.20.cloned.1.call-start = ((), (), s32[]{:S(2)}) async-start(), calls=%async_computation.17 | async-start | bytes 6553600 | tf_op jit(solution)/shard_map/all_gather | solution.py:181
  653.3 2.8 copy-start.5
  655.7 1.9 copy-start.19
  659.8 1.5 copy-start
  663.2 217.2 %reduce-scatter.19.cloned.1.call-start = ((), (), s32[]{:S(2)}) async-start(), calls=%async_computation.18 | async-start | bytes 6553600 | tf_op jit(solution)/shard_map/reduce_scatter | solution.py:187
  761.9 19.0 %copy-start.22 = (bf16[1024,1024]{1,0:T(8,128)(2,1)S(1)}, bf16[1024,1024]{1,0:T(8,128)(2,1)}, u32[]{:S(2)}) copy-start(bf16[1024,1024]{1,0:T(8,128)(2,1)} %all-gather.16.cloned.1.call-done) | copy-start | bytes 6291460
  778.5 2.4 copy-start.27
  788.2 198.5 %all-gather.22.cloned.1.call-start = ((), (), s32[]{:S(2)}) async-start(), calls=%async_computation.19 | async-start | bytes 6553600 | tf_op jit(solution)/shard_map/all_gather | solution.py:196
  880.5 3.5 copy-start.1
  880.5 3.5 copy-start.6
  885.1 1.5 copy-start.2
  888.0 237.5 %reduce-scatter.33.cloned.1.call-start = ((), (), s32[]{:S(2)}) async-start(), calls=%async_computation.26 | async-start | bytes 73728
  888.8 238.0 %reduce-scatter.31.cloned.1.call-start = ((), (), s32[]{:S(2)}) async-start(), calls=%async_computation.25 | async-start | bytes 73728
  991.8 7.3 copy-start.26
  1080.1 10.0 copy-start.23
  1080.1 81.5 %reduce-scatter.23.cloned.1.call-start = ((), (), s32[]{:S(2)}) async-start(), calls=%async_computation.21 | async-start | bytes 3538944 | tf_op jit(solution)/shard_map/reduce_scatter | solution.py:236
  1090.0 167.5 %reduce-scatter.21.cloned.1.call-start = ((), (), s32[]{:S(2)}) async-start(), calls=%async_computation.20 | async-start | bytes 6553600 | tf_op jit(solution)/shard_map/reduce_scatter | solution.py:218
  1098.3 214.8 %reduce-scatter.29.cloned.1.call-start = ((), (), s32[]{:S(2)}) async-start(), calls=%async_computation.24 | async-start | bytes 4718592 | tf_op jit(solution)/shard_map/reduce_scatter | solution.py:240
  1108.9 259.1 %reduce-scatter.27.cloned.1.call-start = ((), (), s32[]{:S(2)}) async-start(), calls=%async_computation.23 | async-start | bytes 4718592 | tf_op jit(solution)/shard_map/reduce_scatter | solution.py:239
  1119.4 138.1 %copy-start.3 = (f32[640,1024]{1,0:T(8,128)S(1)}, f32[640,1024]{1,0:T(8,128)}, u32[]{:S(2)}) copy-start(f32[640,1024]{1,0:T(8,128)} %copy-done.2) | copy-start | bytes 7864324
  1119.5 138.1 %copy-start.9 = (f32[640]{0:T(1024)S(1)}, f32[640]{0:T(1024)}, u32[]{:S(2)}) copy-start(f32[640]{0:T(1024)} %copy-done.8) | copy-start | bytes 7684
  1119.5 288.1 %reduce-scatter.25.cloned.1.call-start = ((), (), s32[]{:S(2)}) async-start(), calls=%async_computation.22 | async-start | bytes 1179648 | tf_op jit(solution)/shard_map/reduce_scatter | solution.py:237
  1125.4 135.5 %copy-start.15 = (f32[1024]{0:T(1024)S(1)}, f32[1024]{0:T(1024)}, u32[]{:S(2)}) copy-start(f32[1024]{0:T(1024)} %get-tuple-element.216) | copy-start | bytes 12292
  1125.4 135.5 %copy-start.16 = (f32[1024]{0:T(1024)S(1)}, f32[1024]{0:T(1024)}, u32[]{:S(2)}) copy-start(f32[1024]{0:T(1024)} %get-tuple-element.221) | copy-start | bytes 12292
  1125.4 135.5 %copy-start.17 = (f32[1024]{0:T(1024)S(1)}, f32[1024]{0:T(1024)}, u32[]{:S(2)}) copy-start(f32[1024]{0:T(1024)} %get-tuple-element.254) | copy-start | bytes 12292
Sparse Core Ops, SparseCore 0:
  9.9 28.2 all-gather.11
  40.4 98.0 all-gather.9
  211.2 176.3 reduce-scatter.14
  389.4 29.1 all-gather.15
  420.6 98.0 all-gather.13
  520.4 26.4 all-gather.17
  561.2 92.1 reduce-scatter.16
  663.3 98.5 all-gather.19
  788.3 92.0 reduce-scatter.18
  888.1 98.5 all-gather.21
  989.7 31.9 reduce-scatter.32
  1080.2 31.8 reduce-scatter.30
  1115.4 46.0 reduce-scatter.22
  1163.7 93.7 reduce-scatter.20
  1261.3 51.7 reduce-scatter.28
  1316.9 51.0 reduce-scatter.26
  1371.5 35.9 reduce-scatter.24
where the time goes:
time: 1430 us; the launch traced here: 1410 us
  waiting for transfers between devices  1010 us (71%)
  matrix products  175 us (12%)
  local copies, waits for them, and re-layouts  89.3 us (6%)
  blocking collectives  70.7 us (5%)
  other arithmetic  55 us (4%)
  between operations  14.5 us (1%)
    reduce_scatter x1, waiting for transfers between devices, body(): lax.psum_scatter(jnp.dot(attn_flat, out_weight, preferred_element_type=jn...  175 us
    all_gather x1, waiting for transfers between devices, body(): h_all = lax.all_gather(h_low, 'mp', axis=0, tiled=True)  100 us
    all_gather x1, waiting for transfers between devices, body(): y_all = lax.all_gather(y_low, 'mp', axis=0, tiled=True)  100 us
    all_gather x1, waiting for transfers between devices, body(): grad_f_all = lax.all_gather(grad_f_low, 'mp', axis=0, tiled=True)  98.6 us
    all_gather x1, waiting for transfers between devices, body(): grad_a_all = lax.all_gather(grad_a_low, 'mp', axis=0, tiled=True)  97.8 us
    reduce_scatter x1, waiting for transfers between devices, body(): lax.psum_scatter(jnp.einsum('tce,cde->td', grad_qkv, qkv_weight, preferre...  94.1 us
    reduce_scatter x1, waiting for transfers between devices, body(): lax.psum_scatter(jnp.dot(grad_pre_low, up_weight, preferred_element_type=...  92.2 us
    reduce_scatter x1, waiting for transfers between devices, body(): lax.psum_scatter(jnp.dot(hidden_low, down_weight, preferred_element_type=...  92 us
  transfers between devices with their start and end apart: 17, of which 14 were waited for; matrix products, arithmetic and copies ran while one was open for 14% of the time, Pallas kernels for 0%

commit v1 on v0

v1 whole, which is shorter than its diff:
```python
import functools
import math

import jax
import jax.numpy as jnp
from jax import lax
from jax.experimental import pallas as pl
from jax.experimental.pallas import tpu as pltpu
from jax.sharding import PartitionSpec as P

BLOCK = 25
TSTEPS = 5000
LN_EPS = 1e-05
MASKED = -1e30
MESH = pl.DeviceIdType.MESH
BF = jnp.bfloat16
F32 = jnp.float32
PIECES = 12
LANES = 4
VMEM_LIMIT = 62 * 2**20


def dot_nn(left, right):
    return lax.dot_general(left, right, (((1,), (0,)), ((), ())), preferred_element_type=F32)


def dot_nt(left, right):
    return lax.dot_general(left, right, (((1,), (1,)), ((), ())), preferred_element_type=F32)


def dot_tn(left, right):
    return lax.dot_general(left, right, (((0,), (0,)), ((), ())), preferred_element_type=F32)


class Place:
    def __init__(self, outer):
        dp = lax.axis_index("dp")
        self.z = lax.axis_index("mp")
        self.outer = outer
        self.own = lax.div(dp, outer)
        self.rest = lax.rem(dp, outer)
        self.core = lax.rem(self.own, 2)
        self.chip = lax.div(self.own, 2)
        col, row = lax.rem(self.chip, 2), lax.div(self.chip, 2)
        self.side = row * 2 + (1 - col)
        self.over = (1 - row) * 2 + col
        self.diag = (1 - row) * 2 + (1 - col)

    def dev(self, chip, core, z):
        return ((chip * 2 + core) * self.outer + self.rest, z)

    def partner(self):
        return self.dev(self.chip, 1 - self.core, self.z)

    def beside(self):
        return self.dev(self.side, self.core, self.z)

    def across(self):
        return self.dev(self.over, self.core, self.z)

    def along(self, k):
        return self.dev(self.chip, self.core, lax.rem(self.z + k, 4))


def greet(at):
    barrier = pltpu.get_barrier_semaphore()
    peers = [at.partner(), at.beside(), at.across()] + [at.along(k) for k in range(1, 4)]
    for peer in peers:
        pl.semaphore_signal(barrier, inc=1, device_id=peer, device_id_type=MESH)
    pl.semaphore_wait(barrier, len(peers))


def wait_for(ref, sem):
    pltpu.make_async_copy(ref, ref, sem).wait()


def send(src, dst, send_sem, recv_sem, device):
    pltpu.make_async_remote_copy(
        src, dst, send_sem, recv_sem, device_id=device, device_id_type=MESH
    ).start()


def when_in(piece, count, action):
    @pl.when(jnp.logical_and(piece >= 0, piece < count))
    def _():
        action(piece)


def gather_kernel(outer, shard, full, own_sem, sent, got_z, got_x, got_y, got_xd, got_yd, got_c):
    at = Place(outer)
    greet(at)
    mine = pltpu.make_async_copy(shard, full.at[:, at.own, at.z], own_sem)
    mine.start()
    x_lane, y_lane, d_lane = at.side * 2 + at.core, at.over * 2 + at.core, at.diag * 2 + at.core

    def first(p):
        src, dst = shard.at[p], full.at[p, at.own, at.z]
        send(src, dst, sent.at[p], got_x.at[p], at.beside())
        send(src, dst, sent.at[p], got_y.at[p], at.across())
        for k in range(1, 4):
            send(src, dst, sent.at[p], got_z.at[p], at.along(k))
        send(src, dst, sent.at[p], got_c.at[p], at.partner())

    def second(p):
        wait_for(full.at[p, at.own, 0:3], got_z.at[p])
        for k in range(1, 4):
            block = full.at[p, at.own, lax.rem(at.z + k, 4)]
            send(block, block, sent.at[p], got_x.at[p], at.beside())
            send(block, block, sent.at[p], got_y.at[p], at.across())
            send(block, block, sent.at[p], got_c.at[p], at.partner())

    def third(p):
        wait_for(full.at[p, x_lane], got_x.at[p])
        block = full.at[p, x_lane, 0:2]
        send(block, block, sent.at[p], got_yd.at[p], at.across())
        block = full.at[p, x_lane]
        send(block, block, sent.at[p], got_c.at[p], at.partner())
        wait_for(full.at[p, y_lane], got_y.at[p])
        block = full.at[p, y_lane, 2:4]
        send(block, block, sent.at[p], got_xd.at[p], at.beside())
        block = full.at[p, y_lane]
        send(block, block, sent.at[p], got_c.at[p], at.partner())

    def fourth(p):
        wait_for(full.at[p, d_lane, 0:2], got_yd.at[p])
        wait_for(full.at[p, d_lane, 2:4], got_xd.at[p])
        block = full.at[p, d_lane]
        send(block, block, sent.at[p], got_c.at[p], at.partner())

    def fifth(p):
        wait_for(full.at[p, 0:4], got_c.at[p])

    first(0)
    first(1)

    def tick(t, carry):
        for action, shift in ((first, 2), (second, 0), (third, -1), (fourth, -2), (fifth, -3)):
            when_in(t + shift, PIECES, action)
        return carry

    lax.fori_loop(0, PIECES + 3, tick, 0)
    mine.wait()

    def drain(p, carry):
        wait_for(full.at[p, 0:7], sent.at[p])
        wait_for(full.at[p, 7, 0:3], sent.at[p])
        return carry

    lax.fori_loop(0, PIECES, drain, 0)


def gather_weights(outer, shard):
    sem = pltpu.SemaphoreType.DMA
    return pl.pallas_call(
        functools.partial(gather_kernel, outer),
        out_shape=jax.ShapeDtypeStruct((PIECES, 8, 4) + shard.shape[1:], BF),
        in_specs=[pl.BlockSpec(memory_space=pl.ANY)],
        out_specs=pl.BlockSpec(memory_space=pl.ANY),
        scratch_shapes=[sem] + [sem((PIECES,))] * 7,
        compiler_params=pltpu.CompilerParams(
            collective_id=1, has_side_effects=True, vmem_limit_bytes=VMEM_LIMIT
        ),
    )(shard)


def scatter_kernel(
    outer, grads, out, part, lane, got_c, got_dx, got_dy, got_x, got_y, got_z,
    load_sem, sent0, sent1, sent2, sent3, sem_c, sem_dx, sem_dy, sem_x, sem_y, sem_z, credit,
):
    at = Place(outer)
    greet(at)

    def load(p):
        return pltpu.make_async_copy(grads.at[p], part.at[lax.rem(p, 2)], load_sem.at[lax.rem(p, 2)])

    def first(p):
        slot = lax.rem(p, 2)
        load(p).wait()

        @pl.when(p >= 2)
        def _():
            pl.semaphore_wait(credit, 1)

        send(part.at[slot, :, 1 - at.core], got_c.at[slot], sent0.at[p], sem_c.at[p], at.partner())

    def second(p):
        slot, row = lax.rem(p, 2), lax.rem(p, LANES)
        wait_for(got_c.at[slot], sem_c.at[p])

        @pl.when(p >= LANES)
        def _():
            wait_for(lane.at[row, 0], sent1.at[p - LANES])
            wait_for(lane.at[row, 0:2], sent2.at[p - LANES])
            wait_for(lane.at[row, 0, 0:3], sent3.at[p - LANES])

        def add(i, carry):
            a, b = lax.div(i, 4), lax.rem(i, 4)
            lane[row, a, b] = part[slot, a, at.core, b] + got_c[slot, a, b]
            return carry

        lax.fori_loop(0, 16, add, 0)

        @pl.when(p < PIECES - 2)
        def _():
            pl.semaphore_signal(credit, inc=1, device_id=at.partner(), device_id_type=MESH)

        wait_for(got_c.at[slot], sent0.at[p])

        @pl.when(p + 2 < PIECES)
        def _():
            load(p + 2).start()

        send(lane.at[row, at.diag, 0:2], got_dy.at[p], sent1.at[p], sem_dy.at[p], at.across())
        send(lane.at[row, at.diag, 2:4], got_dx.at[p], sent1.at[p], sem_dx.at[p], at.beside())

    def third(p):
        row = lax.rem(p, LANES)
        wait_for(got_dy.at[p], sem_dy.at[p])

        def add_y(i, carry):
            lane[row, at.side, i] = lane[row, at.side, i] + got_dy[p, i]
            return carry

        lax.fori_loop(0, 2, add_y, 0)
        send(lane.at[row, at.side], got_x.at[p], sent2.at[p], sem_x.at[p], at.beside())
        wait_for(got_dx.at[p], sem_dx.at[p])

        def add_x(i, carry):
            lane[row, at.over, i + 2] = lane[row, at.over, i + 2] + got_dx[p, i]
            return carry

        lax.fori_loop(0, 2, add_x, 0)
        send(lane.at[row, at.over], got_y.at[p], sent2.at[p], sem_y.at[p], at.across())

    def fourth(p):
        row = lax.rem(p, LANES)
        wait_for(got_x.at[p], sem_x.at[p])
        wait_for(got_y.at[p], sem_y.at[p])

        def add(i, carry):
            total = lane[row, at.chip, i].astype(F32) + got_x[p, i].astype(F32)
            lane[row, at.chip, i] = (total + got_y[p, i].astype(F32)).astype(BF)
            return carry

        lax.fori_loop(0, 4, add, 0)
        for k in range(1, 4):
            block = lane.at[row, at.chip, lax.rem(at.z + k, 4)]
            send(block, got_z.at[p, k - 1], sent3.at[p], sem_z.at[p], at.along(k))

    def fifth(p):
        row = lax.rem(p, LANES)
        wait_for(got_z.at[p], sem_z.at[p])
        total = lane[row, at.chip, at.z].astype(F32)
        for k in range(3):
            total = total + got_z[p, k].astype(F32)
        out[p] = total

    load(0).start()
    load(1).start()

    def tick(t, carry):
        for action, shift in ((first, 0), (second, -1), (third, -2), (fourth, -3), (fifth, -4)):
            when_in(t + shift, PIECES, action)
        return carry

    lax.fori_loop(0, PIECES + 4, tick, 0)
    for p in range(PIECES - LANES, PIECES):
        row = p % LANES
        wait_for(lane.at[row, 0], sent1.at[p])
        wait_for(lane.at[row, 0:2], sent2.at[p])
        wait_for(lane.at[row, 0, 0:3], sent3.at[p])


def scatter_grads(outer, grads):
    sem = pltpu.SemaphoreType.DMA
    rows, cols = grads.shape[-2:]
    return pl.pallas_call(
        functools.partial(scatter_kernel, outer),
        out_shape=jax.ShapeDtypeStruct((PIECES, rows, cols), F32),
        in_specs=[pl.BlockSpec(memory_space=pl.ANY)],
        out_specs=pl.BlockSpec(memory_space=pltpu.VMEM),
        scratch_shapes=[
            pltpu.VMEM((2, 4, 2, 4, rows, cols), BF),
            pltpu.VMEM((LANES, 4, 4, rows, cols), BF),
            pltpu.VMEM((2, 4, 4, rows, cols), BF),
            pltpu.VMEM((PIECES, 2, rows, cols), BF),
            pltpu.VMEM((PIECES, 2, rows, cols), BF),
            pltpu.VMEM((PIECES, 4, rows, cols), BF),
            pltpu.VMEM((PIECES, 4, rows, cols), BF),
            pltpu.VMEM((PIECES, 3, rows, cols), BF),
            sem((2,)),
        ]
        + [sem((PIECES,))] * 10
        + [pltpu.SemaphoreType.REGULAR],
        compiler_params=pltpu.CompilerParams(
            collective_id=2, has_side_effects=True, vmem_limit_bytes=VMEM_LIMIT
        ),
    )(grads)


def layer_norm(values_in, gain, shift):
    average = jnp.mean(values_in, axis=-1, keepdims=True)
    centred = values_in - average
    variance = jnp.mean(centred * centred, axis=-1, keepdims=True)
    return centred * lax.rsqrt(variance + LN_EPS) * gain + shift


def gelu_exact(values_in):
    return jax.nn.gelu(values_in, approximate=False)


def probs_of(record):
    queries, key_rows, values, usable = record
    scores = jnp.einsum("qhd,khd->hqk", queries, key_rows, preferred_element_type=F32)
    scores = scores * (1.0 / math.sqrt(queries.shape[-1]))
    scores = jnp.where(usable[None], scores, MASKED)
    row_max = jnp.max(scores, axis=-1, keepdims=True)
    expo = jnp.exp(scores - row_max)
    return expo / jnp.sum(expo, axis=-1, keepdims=True)


def attend(record):
    probs = probs_of(record)
    mixed = jnp.einsum("hqk,khd->qhd", probs.astype(BF), record[2], preferred_element_type=F32)
    return mixed.astype(BF)


def attend_back(record):
    queries, key_rows, values, usable, grad_out = record
    probs = probs_of(record[:4])
    scale = 1.0 / math.sqrt(queries.shape[-1])
    grad_v = jnp.einsum("hqk,qhd->khd", probs.astype(BF), grad_out, preferred_element_type=F32)
    grad_p = jnp.einsum("qhd,khd->hqk", grad_out, values, preferred_element_type=F32)
    inner = jnp.sum(probs * grad_p, axis=-1, keepdims=True)
    grad_s = (probs * (grad_p - inner)).astype(BF)
    grad_q = jnp.einsum("hqk,khd->qhd", grad_s, key_rows, preferred_element_type=F32) * scale
    grad_k = jnp.einsum("hqk,qhd->khd", grad_s, queries, preferred_element_type=F32) * scale
    return grad_q.astype(BF), grad_k, grad_v


def body(
    outer, tokens, context, timestep, time_weight, time_bias, qkv_weight, qv_bias, out_weight, out_bias,
    gain_one, shift_one, up_weight, up_bias, down_weight, down_bias, gain_two, shift_two, cotangent,
):
    z = lax.axis_index("mp")
    rows, model = tokens.shape
    seqs = context.shape[0]
    seq_len = rows * 4 // seqs
    dp_size = lax.axis_size("dp")
    groups = None
    if outer > 1:
        groups = [[i * outer + j for j in range(outer)] for i in range(8)]
        qkv_weight, out_weight, up_weight, down_weight = (
            lax.all_gather(w, "dp", axis=1, tiled=True, axis_index_groups=groups)
            for w in (qkv_weight, out_weight, up_weight, down_weight)
        )
    shard = jnp.concatenate(
        [
            qkv_weight.reshape(3, -1, 2, 128).transpose(0, 2, 1, 3).reshape(3, 256, 128),
            out_weight.reshape(1, 256, 128),
            up_weight.reshape(4, 256, 128),
            down_weight.reshape(4, 256, 128),
        ]
    )
    full = gather_weights(outer, shard)
    w_qkv = full[0:3].reshape(3, 8, 4, 2, 128, 128).transpose(0, 1, 4, 2, 3, 5).reshape(3, model, model)
    w_out = full[3].transpose(1, 2, 0, 3).reshape(model, model)
    w_up = full[4:8].transpose(2, 0, 3, 1, 4).reshape(4 * model, model)
    w_down = full[8:12].transpose(2, 0, 3, 1, 4).reshape(4 * model, model)
    qv_bias = lax.all_gather(lax.all_gather(qv_bias, "dp", axis=1, tiled=True), "mp", axis=0, tiled=True)
    up_bias_all = lax.all_gather(lax.all_gather(up_bias, "dp", axis=1, tiled=True), "mp", axis=0, tiled=True)
    heads, head = qv_bias.shape[0], qv_bias.shape[1] // 2
    row_ids = z * rows + jnp.arange(rows, dtype=jnp.int32)
    owner = (row_ids // seq_len)[:, None] == jnp.arange(seqs, dtype=jnp.int32)[None, :]
    fraction = jnp.sum(jnp.where(owner, (timestep.astype(F32) / TSTEPS)[None, :], 0.0), axis=1)
    h_zero = tokens.astype(F32) + fraction[:, None] * time_weight + time_bias
    h_low = h_zero.astype(BF)
    h_all = lax.all_gather(h_low, "mp", axis=0, tiled=True)
    h_win = lax.dynamic_slice(h_all, (z * seq_len, 0), (2 * seq_len, model))
    bias_f = qv_bias.astype(F32)
    queries = (jnp.dot(h_low, w_qkv[0], preferred_element_type=F32) + bias_f[:, :head].reshape(-1)).astype(BF)
    keys = jnp.dot(h_win, w_qkv[1], preferred_element_type=F32).astype(BF)
    values = (jnp.dot(h_win, w_qkv[2], preferred_element_type=F32) + bias_f[:, head:].reshape(-1)).astype(BF)
    step = rows // 5
    live = context + BLOCK
    live_two = lax.dynamic_slice(live, (z,), (2,))
    q_blocks = queries.reshape(5, step, heads, head)
    slots = (z + jnp.arange(5)) // 4
    k_two, v_two = keys.reshape(2, seq_len, heads, head), values.reshape(2, seq_len, heads, head)

    def record_of(j):
        slot = slots[j]
        usable = jnp.broadcast_to(jnp.arange(seq_len)[None, :] < live_two[slot], (step, seq_len))
        return q_blocks[j], k_two[slot], v_two[slot], usable

    attn = lax.map(lambda j: attend(record_of(j)), jnp.arange(5)).reshape(rows, model)
    branch_a = jnp.dot(attn, w_out, preferred_element_type=F32) + out_bias
    y_one, ln_one_back = jax.vjp(layer_norm, h_zero + branch_a, gain_one, shift_one)
    y_low = y_one.astype(BF)
    pre = dot_nt(y_low, w_up) + up_bias_all.reshape(-1).astype(F32)
    hidden, gelu_back = jax.vjp(gelu_exact, pre)
    hidden_low = hidden.astype(BF)
    branch_f = jnp.dot(hidden_low, w_down, preferred_element_type=F32) + down_bias
    y_two, ln_two_back = jax.vjp(layer_norm, y_one + branch_f, gain_two, shift_two)
    layer_out = y_two.astype(BF)
    grad_z2, grad_gain_two, grad_shift_two = ln_two_back(cotangent.astype(F32))
    grad_f = grad_z2.astype(BF)
    grad_down_bias = jnp.sum(grad_f.astype(F32), axis=0)
    (grad_pre,) = gelu_back(dot_nt(grad_f, w_down))
    grad_pre = grad_pre.astype(BF)
    grad_up = dot_tn(grad_pre, y_low).astype(BF)
    grad_down = dot_tn(hidden_low, grad_f).astype(BF)
    grad_up_bias = jnp.sum(grad_pre.astype(F32), axis=0).reshape(up_bias_all.shape)
    grad_y1 = grad_z2 + jnp.dot(grad_pre, w_up, preferred_element_type=F32)
    grad_z1, grad_gain_one, grad_shift_one = ln_one_back(grad_y1)
    grad_a = grad_z1.astype(BF)
    grad_out_bias = jnp.sum(grad_a.astype(F32), axis=0)
    grad_attn = dot_nt(grad_a, w_out).astype(BF)
    grad_out_w = dot_tn(attn, grad_a).astype(BF)
    ga = grad_attn.reshape(5, step, heads, head)

    def back(carry, j):
        dk, dv = carry
        slot = slots[j]
        dq, dk_j, dv_j = attend_back(record_of(j) + (ga[j],))
        return (dk.at[slot].add(dk_j), dv.at[slot].add(dv_j)), dq

    zero = jnp.zeros((2, seq_len, heads, head), F32)
    (dk, dv), dq = lax.scan(back, (zero, zero), jnp.arange(5))
    dq = dq.reshape(rows, model)
    dk, dv = dk.astype(BF).reshape(-1, model), dv.astype(BF).reshape(-1, model)
    grad_qkv = jnp.stack([dot_tn(h_low, dq), dot_tn(h_win, dk), dot_tn(h_win, dv)]).astype(BF)
    grad_qv_bias = jnp.concatenate(
        [
            jnp.sum(dq.astype(F32), axis=0).reshape(heads, head),
            jnp.sum(dv.astype(F32), axis=0).reshape(heads, head),
        ],
        axis=1,
    )
    dh_win = dot_nt(dk, w_qkv[1]) + dot_nt(dv, w_qkv[2])
    dh_all = lax.dynamic_update_slice(jnp.zeros((4 * rows, model), F32), dh_win, (z * seq_len, 0))
    grad_tokens = (
        grad_z1
        + dot_nt(dq, w_qkv[0])
        + lax.psum_scatter(dh_all.astype(BF), "mp", scatter_dimension=0, tiled=True).astype(F32)
    )
    grad_time_weight = jnp.sum(fraction[:, None] * grad_tokens, axis=0)
    grad_time_bias = jnp.sum(grad_tokens, axis=0)
    parts = jnp.concatenate(
        [
            grad_qkv.reshape(3, 8, 128, 4, 2, 128).transpose(0, 1, 3, 4, 2, 5).reshape(3, 8, 4, 256, 128),
            grad_out_w.reshape(1, 4, 256, 8, 128).transpose(0, 3, 1, 2, 4),
            grad_up.reshape(4, 4, 256, 8, 128).transpose(1, 3, 0, 2, 4),
            grad_down.reshape(4, 4, 256, 8, 128).transpose(1, 3, 0, 2, 4),
        ]
    )
    done = scatter_grads(outer, parts.reshape(PIECES, 4, 2, 4, 256, 128))
    weight_grads = (
        done[0:3].reshape(3, 2, 128, 128).transpose(0, 2, 1, 3).reshape(3, 128, 256),
        done[3],
        done[4:8].reshape(1024, 128),
        done[8:12].reshape(1024, 128),
    )
    if outer > 1:
        weight_grads = tuple(
            lax.psum_scatter(g, "dp", scatter_dimension=1, tiled=True, axis_index_groups=groups)
            for g in weight_grads
        )
    grad_qkv, grad_out_w, grad_up, grad_down = weight_grads
    small = [
        lax.psum_scatter(v, ("dp", "mp"), scatter_dimension=0, tiled=True)
        for v in (
            grad_out_bias, grad_gain_one, grad_shift_one, grad_gain_two, grad_shift_two, grad_down_bias,
            grad_time_weight, grad_time_bias,
        )
    ]
    grad_qv_bias = lax.psum(grad_qv_bias, ("dp", "mp"))
    grad_up_bias = lax.psum(grad_up_bias, ("dp", "mp"))
    dp = lax.axis_index("dp")
    grad_qv_bias = lax.dynamic_slice(
        grad_qv_bias, (z * (heads // 4), dp * (2 * head // dp_size)), (heads // 4, 2 * head // dp_size)
    )
    n_up, w_upb = up_bias_all.shape
    grad_up_bias = lax.dynamic_slice(
        grad_up_bias, (z * (n_up // 4), dp * (w_upb // dp_size)), (n_up // 4, w_upb // dp_size)
    )
    return (
        layer_out, grad_tokens, small[6], small[7], grad_qkv, grad_qv_bias,
        grad_out_w, small[0], small[1], small[2], grad_up, grad_up_bias,
        grad_down, small[5], small[3], small[4],
    )


def solution(mesh):
    outer = mesh.shape["dp"] // 8
    placed = (
        P(("dp", "mp"), None), P("dp"), P("dp"), P(), P(), P(None, "dp", "mp"), P("mp", "dp"), P("mp", "dp"),
        P(), P(), P(), P("mp", "dp"), P("mp", "dp"), P("mp", "dp"), P(), P(), P(), P(("dp", "mp"), None),
    )
    spread = P(("dp", "mp"))
    wide = P("mp", "dp")
    return jax.shard_map(
        functools.partial(body, outer),
        mesh=mesh,
        in_specs=placed,
        out_specs=(
            P(("dp", "mp"), None), P(("dp", "mp"), None), spread, spread, P(None, "dp", "mp"), wide, wide,
            spread, spread, spread, wide, wide, wide, spread, spread, spread,
        ),
        check_vma=False,
    )
```

time: 1430 us -> 907 us (0.63)
  waiting for transfers between devices: 1010 us -> 0.07 us
  Pallas kernels: 0 us -> 278 us
  local copies, waits for them, and re-layouts: 89.3 us -> 209 us
  loops' own time: 0.35 us -> 39.5 us
  matrix products: 175 us -> 206 us
    reduce_scatter x8 -> x1, waiting for transfers between devices: 588 us -> 0.02 us  [body(): lax.psum_scatter(dh_all.astype(BF), 'mp', scatter_dimension=0, tiled=True)]
    all_gather x6 -> x0, waiting for transfers between devices: 319 us -> none  [the longest x1 100 us: body(): y_all = lax.all_gather(y_low, 'mp', axis=0, tiled=True)]
    pallas_call x0 -> x2, Pallas kernels: none -> 278 us  [the longest x1 160 us: gather_weights(): pl.pallas_call(functools.partial(gather_kernel, outer), out_shape=jax.Sha...]
    all_gather x1, waiting for transfers between devices: 100 us -> 0.02 us  [body(): h_all = lax.all_gather(h_low, 'mp', axis=0, tiled=True)]
    transpose x0 -> x5, local copies, waits for them, and re-layouts: none -> 43.8 us  [the longest x2 25.6 us: body(): w_down = full[8:12].transpose(2, 0, 3, 1, 4).reshape(4 * model, model)]
    another operation x2, loops' own time: 0.35 us -> 39.5 us  [the longest x1 19.9 us: body(): (dk, dv), dq = lax.scan(back, (zero, zero), jnp.arange(5))]
    dot_general x47 -> x53, matrix products: 175 us -> 206 us  [the longest x6 66 us: dot_nt(): lax.dot_general(left, right, (((1,), (1,)), ((), ())), preferred_element_...]
    unnamed x70 -> x150, local copies, waits for them, and re-layouts: 17.9 us -> 40.4 us
  transfers between devices with their start and end apart: 17 -> 2, of which waited for: 14 -> 0; matrix products, arithmetic and copies ran while one was open for 14% -> 20% of each run, Pallas kernels for 0% -> 31%
where the time goes in v1:
time: 907 us; the launch traced here: 900 us
  Pallas kernels  278 us (31%)
  local copies, waits for them, and re-layouts  209 us (23%)
  matrix products  206 us (23%)
  blocking collectives  83.5 us (9%)
  other arithmetic  68.6 us (8%)
  loops' own time  39.5 us (4%)
  between operations  15.2 us (2%)
    pallas_call x1, Pallas kernels, gather_weights(): pl.pallas_call(functools.partial(gather_kernel, outer), out_shape=jax.Sha...  160 us
    pallas_call x1, Pallas kernels, scatter_grads(): pl.pallas_call(functools.partial(scatter_kernel, outer), out_shape=jax.Sh...  118 us
    dot_general x6, matrix products, dot_nt(): lax.dot_general(left, right, (((1,), (1,)), ((), ())), preferred_element_...  66 us
    unnamed x150, local copies, waits for them, and re-layouts  40.4 us
    unnamed x1, blocking collectives  40.3 us
    dot_general x6, matrix products, dot_tn(): lax.dot_general(left, right, (((0,), (0,)), ((), ())), preferred_element_...  30.5 us
    transpose x2, local copies, waits for them, and re-layouts, body(): w_down = full[8:12].transpose(2, 0, 3, 1, 4).reshape(4 * model, model)  25.6 us
    dot_general x5, matrix products, attend_back(): jnp.einsum('hqk,qhd->khd', grad_s, queries, preferred_element_type=F32)  20.8 us
  transfers between devices with their start and end apart: 2, of which 0 were waited for; matrix products, arithmetic and copies ran while one was open for 20% of the time, Pallas kernels for 31%

profile of v1, /device:TPU:0, one launch (start us, length us, event | category | flops | bytes accessed | tf_op | source)
XLA Modules:
  0.0 900.3 jit_solution(684498296379270364)
XLA Ops:
  8.2 2.8 fusion.79
  12.1 159.9 %shard_map.297 = bf16[12,8,4,256,128]{4,3,2,1,0:T(8,128)(2,1)} custom-call(bf16[12,256,128]{2,1,0:T(8,128)(2,1)} %pad_maximum_fusion.2.shard), custom_call_target="tpu_custom_call" | custom-call | tf_op jit(solution)/shard_map/pallas_call | solution.py:154
  172.0 6.3 slice.93
  178.4 9.0 %copy.108 = bf16[3,8,4,2,128,128]{4,1,5,3,2,0:T(8,128)(2,1)} copy(bf16[3,8,4,2,128,128]{5,4,3,2,1,0:T(8,128)(2,1)} %bitcast.355) | data formatting | bytes 12582912 | tf_op jit(solution)/shard_map/reshape | solution.py:366
  187.4 9.0 all-gather
  196.4 12.9 %all-gather.1 = bf16[4,4,128]{2,1,0:T(4,128)(2,1)S(1)} all-gather(bf16[1,4,128]{2,1,0:T(4,128)(2,1)S(1)} %bitcast.398), channel_id=1, replica_groups=mesh['dp'=8,'mp'=4] {'mp'}, dimensions={0}, use_global_device_ids=true | all-gather | bytes 5120 | tf_op jit(solution)/shard_map/all_gather | solution.py:370
  209.6 5.6 fusion.150
  216.5 2.6 add_convert_fusion.3
  219.1 3.6 reshape.392
  222.7 3.6 copy.114
  228.0 2.7 copy.117
  230.8 11.8 %slice_bitcast_fusion = (bf16[4,4,256,8,128]{4,2,0,3,1:T(8,128)(2,1)}, bf16[4,4,256,8,128]{4,2,0,3,1:T(8,128)(2,1)}) fusion(bf16[12,8,4,256,128]{4,3,2,1,0:T(8,128)(2,1)} %shard_map.297), kind=kLoop, calls=%fused_computation.98 | loop fusion | bytes 33554432 | tf_op jit(solution)/shard_map/transpose | solution.py:369
  242.6 13.7 %copy.118 = bf16[4,4,256,8,128]{4,3,2,1,0:T(8,128)(2,1)} copy(bf16[4,4,256,8,128]{4,2,0,3,1:T(8,128)(2,1)} %get-tuple-element.296) | data formatting | bytes 16777216 | tf_op jit(solution)/shard_map/transpose | solution.py:368
  256.3 9.4 %all-gather.2 = bf16[8,16,8]{1,2,0:T(8,128)(2,1)S(1)} all-gather(bf16[1,16,8]{1,2,0:T(8,128)(2,1)S(1)} %bitcast.399), channel_id=1, replica_groups=mesh['dp'=8,'mp'=4] {'dp'}, dimensions={0}, use_global_device_ids=true | all-gather | bytes 2304 | tf_op jit(solution)/shard_map/all_gather | solution.py:371
  265.8 13.8 %copy.120 = bf16[4,4,256,8,128]{4,3,2,1,0:T(8,128)(2,1)} copy(bf16[4,4,256,8,128]{4,2,0,3,1:T(8,128)(2,1)} %get-tuple-element.295) | data formatting | bytes 16777216 | tf_op jit(solution)/shard_map/transpose | solution.py:369
  279.7 11.9 %all_gather.19 = bf16[32,128]{1,0:T(8,128)(2,1)S(1)} all-gather(bf16[8,128]{1,0:T(8,128)(2,1)S(1)} %bitcast.397), channel_id=1, replica_groups=mesh['dp'=8,'mp'=4] {'mp'}, dimensions={0}, use_global_device_ids=true | all-gather | bytes 10240 | tf_op jit(solution)/shard_map/all_gather | solution.py:371
  291.7 4.6 add_convert_fusion.1
  296.3 4.2 reshape.391
  300.5 5.5 copy.113
  306.0 4.6 fusion.99
  310.5 4.0 reshape.393
  314.6 4.5 copy.115
  320.4 56.2 %while.26 = (s32[]{:T(128)}, bf16[5,128,16,64]{1,3,2,0:T(8,128)(2,1)}, s32[5]{0:T(128)S(1)}, s32[5]{0:T(128)S(1)}, bf16[2,512,16,64]{1,3,2,0:T(8,128)(2,1)}, /*i...) while((s32[]{:T(128)}, ...), condition=%wide.region_4.5_spmd, body=%wide.region_1.4_spmd.sunk | while | flops 276956160 | bytes 27805448 | solution.py:396
  376.6 2.6 copy.116
  384.4 32.3 %multiply_convert_fusion.1 = (bf16[640,4096]{1,0:T(8,128)(2,1)S(1)}, f32[640,4096]{1,0:T(8,128)}, f32[640,4096]{1,0:T(8,128)}) fusion(f32[4096]{0:T(1024)S(1)} %bitcast_convert_fusion, bf16[512,8,8,128]{3,2,1,0:T(8,128)(2,1)S(1)} %bitcast.360, f32[640,1024]{1,0:T(8,128)S(1)} %get-tuple-element.306, f32[1024]{0:T(1024)S(1)} %copy-done.58, ...), kind=kOutput, calls=%fused_computation.74 | convolution fusion | flops 5545000960 | bytes 37254144 | tf_op jit(solution)/shard_map/dot_general | solution.py:28
  416.8 5.8 fusion.154
  431.0 19.0 %convert_reduce_fusion = (f32[4096]{0:T(1024)}, bf16[640,4096]{1,0:T(8,128)(2,1)}) fusion(f32[640,4096]{1,0:T(8,128)} %get-tuple-element.288, bf16[640,1024]{1,0:T(8,128)(2,1)} %get-tuple-element.278, bf16[512,8,8,128]{3,2,1,0:T(8,128)(2,1)} %bitcast.361, f32[640,4096]{1,0:T(8,128)} %get-tuple-element.307, f32[4096]{0:T(1024)S(1)} %bitcast_convert_fusion), kind=kOutput, calls=%fused_computation.72 | convolution fusion | flops 5413269504 | bytes 35946496 | tf_op jit(solution)/shard_map/dot_general | solution.py:28
  450.1 12.5 %multiply_reduce_fusion.1 = (f32[1024]{0:T(1024)}, f32[640]{0:T(1024)S(1)}, f32[1024]{0:T(1024)}, f32[640,1024]{1,0:T(8,128)S(1)}) fusion(f32[640,1024]{1,0:T(8,128)S(1)} %get-tuple-element.306, f32[640]{0:T(1024)S(1)} %fusion.138, f32[640]{0:T(1024)S(1)} %broadcast_multiply_fusion.1, f32[1024]{0:T(1024)S(1)} %copy-done.50, ...), kind=kOutput, calls=%fused_computation.118 | convolution fusion | flops 5375260160 | bytes 21518336 | tf_op jit(solution)/shard_map/dot_general | solution.py:414
  467.1 2.6 fusion.114
  469.7 4.4 reshape.390
  474.1 4.7 copy.124
  478.8 2.5 broadcast_in_dim.96
  481.3 2.5 broadcast_in_dim.96.clone
  485.2 107.8 %while.27 = (s32[]{:T(128)}, f32[2,512,16,64]{1,3,2,0:T(8,128)}, f32[2,512,16,64]{1,3,2,0:T(8,128)}, bf16[5,128,16,64]{1,3,2,0:T(8,128)(2,1)}, s32[5]{0:T(128)S(...) while((s32[]{:T(128)}, f32[2,512,16,64]{1,3,2,0:T(8,128)}, ...), condition=%wide.region_18.19_spmd, body=%wide.region_13.18_spmd.sunk | while | flops 689699840 | bytes 94688648 | solution.py:429
  495.4 2.5 fusion.213
  501.0 4.2 fusion.212
  517.0 2.5 fusion.213
  522.6 4.2 fusion.212
  538.6 2.5 fusion.213
  544.1 4.2 fusion.212
  560.1 2.5 fusion.213
  565.7 4.2 fusion.212
  581.6 2.5 fusion.213
  587.2 4.1 fusion.212
  593.1 2.5 convert_reduce_fusion.1
  598.3 3.3 convert_element_type.133
  605.4 2.4 fusion.85
  607.9 3.0 broadcast_in_dim.97
  610.8 3.9 add_dynamic-update-slice_fusion
  621.1 2.9 copy.137
  624.0 2.6 copy.126
  631.0 9.5 %convert_bitcast_fusion.1 = bf16[512,8,8,128]{3,1,2,0:T(8,128)(2,1)} fusion(bf16[640,4096]{1,0:T(8,128)(2,1)S(1)} %bitcast.402, f32[640,1024]{1,0:T(8,128)S(1)} %copy-done.5, f32[1024]{0:T(1024)S(1)} %copy-done.59, f32[1024]{0:T(1024)S(1)} %copy-done.50, f32[640]{0:T(1024)S(1)} %fusion.138, f32[640]{0:T(1024)S(1)} %broadcast_multiply_fusion.1), kind=kOutput, calls=%fused_computation.97 | convolution fusion | flops 5376180224 | bytes 16266240 | tf_op jit(solution)/shard_map/dot_general | solution.py:32
  640.5 8.8 copy.166
  649.3 8.9 copy.133
  658.3 11.9 %convert_bitcast_fusion = bf16[512,8,8,128]{3,1,2,0:T(8,128)(2,1)} fusion(bf16[640,4096]{1,0:T(8,128)(2,1)} %copy-done.63, bf16[640,1024]{1,0:T(8,128)(2,1)S(1)} %copy-done.29), kind=kOutput, calls=%fused_computation.96 | convolution fusion | flops 5372903424 | bytes 14942208 | tf_op jit(solution)/shard_map/dot_general | solution.py:32
  670.2 8.8 copy.167
  679.0 8.9 copy.134
  690.1 2.6 convert_bitcast_fusion.3
  692.7 2.6 convert_bitcast_fusion.4
  695.4 3.4 pad_maximum_fusion.1
  698.8 16.9 %pad_maximum_fusion.grads = bf16[12,4,2,4,256,128]{5,4,3,2,1,0:T(8,128)(2,1)} fusion(bf16[4,4,2,4,256,128]{5,4,3,2,1,0:T(8,128)(2,1)} %bitcast.352, bf16[4,4,2,4,256,128]{5,4,3,2,1,0:T(8,128)(2,1)} %bitcast.351, bf16[1,4,2,4,256,128]{5,4,3,2,1,0:T(8,128)(2,1)S(1)} %bitcast.356, bf16[3,4,2,4,256,128]{5,4,3,2,1,0:T(8,128)(2,1)} %bitcast.354), kind=kLoop, calls=%fused_computation.69 | loop fusion | flops 37748736 | bytes 50331648 | tf_op jit(solution)/shard_map/concatenate | solution.py:449
  715.7 117.9 %shard_map.298 = f32[12,256,128]{2,1,0:T(8,128)} custom-call(bf16[12,4,2,4,256,128]{5,4,3,2,1,0:T(8,128)(2,1)} %pad_maximum_fusion.grads), custom_call_target="tpu_custom_call" | custom-call | tf_op jit(solution)/shard_map/pallas_call | solution.py:277
  841.2 5.7 fusion.144
  846.9 40.3 %all-reduce.8 = (f32[1024]{0:T(1024)S(1)}, f32[1024]{0:T(1024)S(1)}, f32[16,128]{1,0:T(8,128)S(1)}, f32[1024]{0:T(1024)S(1)}, f32[1024]{0:T(1024)S(1)}, /*index=...) all-reduce(f32[1024]{0:T(1024)S(1)} %get-tuple-element.227, ...), channel_id=3, replica_groups=mesh['dp'=8,'mp'=4] {'dp','mp'}, use_global_device_ids=true, to_apply=%region_21.22.clone | all-reduce | flops 14336 | bytes 114688
  (332 shorter events, 150.5 us)
Async XLA Ops:
  7.2 3.9 copy-start
  7.2 3.9 copy-start.34
  7.2 3.9 copy-start.33
  7.2 3.9 copy-start.32
  7.2 284.5 %all-gather.5.cloned.1.call-start = ((), (), s32[]{:S(2)}) async-start(), calls=%async_computation.1 | async-start | bytes 6553600 | tf_op jit(solution)/shard_map/all_gather | solution.py:378
  8.1 371.1 %copy-start.35 = (f32[640]{0:T(1024)}, f32[640]{0:T(1024)S(1)}, u32[]{:S(2)}) copy-start(f32[640]{0:T(1024)S(1)} %select_reduce_fusion) | copy-start | bytes 7684
  11.0 830.1 %reduce-scatter.2.cloned.1.call-start = ((), (), s32[]{:S(2)}) async-start(), calls=%async_computation.2 | async-start | bytes 6553600 | tf_op jit(solution)/shard_map/reduce_scatter | solution.py:445
  178.4 9.0 %copy-start.55 = (bf16[4,16]{1,0:T(4,128)(2,1)S(1)}, bf16[4,16]{1,0:T(4,128)(2,1)}, u32[]{:S(2)}) copy-start(bf16[4,16]{1,0:T(4,128)(2,1)} %param.32) | copy-start | bytes 388
  209.6 6.9 copy-start.11
  242.6 13.7 %copy-start.54 = (bf16[8,16]{1,0:T(8,128)(2,1)S(1)}, bf16[8,16]{1,0:T(8,128)(2,1)}, u32[]{:S(2)}) copy-start(bf16[8,16]{1,0:T(8,128)(2,1)} %param.38) | copy-start | bytes 772
  265.8 13.8 %copy-start.60 = (s32[5]{0:T(128)S(1)}, s32[5]{0:T(128)}, u32[]{:S(2)}) copy-start(s32[5]{0:T(128)} %param.27) | copy-start | bytes 64
  320.4 58.8 %copy-start.39 = (f32[1024]{0:T(1024)S(1)}, f32[1024]{0:T(1024)}, u32[]{:S(2)}) copy-start(f32[1024]{0:T(1024)} %param.29) | copy-start | bytes 12292
  320.4 58.8 %copy-start.56 = (f32[1024]{0:T(1024)S(1)}, f32[1024]{0:T(1024)}, u32[]{:S(2)}) copy-start(f32[1024]{0:T(1024)} %param.34) | copy-start | bytes 12292
  376.6 2.6 copy-start.61
  376.6 2.6 copy-start.9
  376.6 2.6 copy-start.15
  376.6 2.6 copy-start.37
  379.2 2.9 slice-start
  379.3 5.1 slice-start.1
  379.3 37.4 %slice-start.2 = ((s8[8388608]{0:T(1024)(128)(4,1)}), s8[4194304]{0:T(1024)(128)(4,1)S(1)}, s32[]{:S(2)}) async-start(s8[8388608]{0:T(1024)(128)(4,1)} %bitcast.362), calls=%async_computation.5 | async-start | bytes 8388608
  381.3 81.3 %copy-start.4 = (f32[640,1024]{1,0:T(8,128)}, f32[640,1024]{1,0:T(8,128)S(1)}, u32[]{:S(2)}) copy-start(f32[640,1024]{1,0:T(8,128)S(1)} %get-tuple-element.306) | copy-start | bytes 7864324
  381.3 3.1 copy-start.50
  381.3 3.1 copy-start.58
  384.4 32.3 %slice-start.3 = ((s8[8388608]{0:T(1024)(128)(4,1)}), s8[4194304]{0:T(1024)(128)(4,1)S(1)}, s32[]{:S(2)}) async-start(s8[8388608]{0:T(1024)(128)(4,1)} %bitcast.362), calls=%async_computation.6 | async-start | bytes 8388608
  384.4 32.3 %copy-start.57 = (f32[1024]{0:T(1024)S(1)}, f32[1024]{0:T(1024)}, u32[]{:S(2)}) copy-start(f32[1024]{0:T(1024)} %param.40) | copy-start | bytes 12292
  416.7 5.9 copy-start.63
  423.0 2.4 copy-start.51
  463.5 3.6 copy-start.16
  463.5 6.2 copy-start.47
  481.3 4.0 copy-start.49
  481.3 4.0 copy-start.62
  493.3 2.2 copy-start.2
  495.4 2.5 copy-start.14
  497.9 2.3 copy-start.3
  517.0 2.5 copy-start.14
  519.5 2.3 copy-start.3
  538.5 2.5 copy-start.14
  541.1 2.3 copy-start.3
  560.1 2.5 copy-start.14
  562.6 2.3 copy-start.3
  581.6 2.5 copy-start.14
  584.1 2.3 copy-start.3
  598.3 12.5 %copy-start.17 = (bf16[128,8,2,512]{3,1,2,0:T(8,128)(2,1)}, bf16[128,8,2,512]{3,1,2,0:T(8,128)(2,1)S(1)}, u32[]{:S(2)}) copy-start(bf16[128,8,2,512]{3,1,2,0:T(8,128)(2,1)S(1)} %copy.163) | copy-start | bytes 6291460
  604.3 3.5 copy-start.19
  607.9 3.0 copy-start.25
  624.0 2.8 copy-start.23
  624.0 2.8 copy-start.31
  624.0 5.8 slice-start.4
  626.8 61.1 %copy-start.28 = (bf16[128,8,5,128]{3,1,2,0:T(8,128)(2,1)}, bf16[128,8,5,128]{3,1,2,0:T(8,128)(2,1)S(1)}, u32[]{:S(2)}) copy-start(bf16[128,8,5,128]{3,1,2,0:T(8,128)(2,1)S(1)} %copy.257) | copy-start | bytes 3932164
  626.8 3.0 slice-start.5
  649.3 8.9 copy-start.29
  679.0 8.9 copy-start.27
  687.9 2.2 copy-start.21
  690.1 2.6 copy-start.20
  833.6 7.5 copy-start.7
  833.6 7.5 copy-start.48
  841.0 5.8 copy-start.41
  841.1 5.8 copy-start.43
  841.1 5.8 copy-start.44
  841.1 5.9 copy-start.45
  841.1 5.9 copy-start.46
  841.1 5.9 copy-start.52
  841.1 5.9 copy-start.53
  841.1 52.1 %copy-start.1 = (bf16[3,128,256]{2,1,0:T(8,128)(2,1)S(1)}, bf16[3,128,256]{2,1,0:T(8,128)(2,1)}, u32[]{:S(2)}) copy-start(bf16[3,128,256]{2,1,0:T(8,128)(2,1)} %param.31) | copy-start | bytes 589828
  (24 other events, 39.5 us)
Sparse Core Ops, SparseCore 0:
  11.1 159.3 all-gather.4
  614.9 91.3 reduce-scatter.1

commit v2 on v1

v2 whole, which is shorter than its diff:
```python
import functools

import jax
import jax.numpy as jnp
from jax import lax
from jax.experimental import pallas as pl
from jax.experimental.pallas import tpu as pltpu
from jax.sharding import PartitionSpec as P

BLOCK = 25
TSTEPS = 5000
LN_EPS = 1e-05
MASKED = -1e30
MESH = pl.DeviceIdType.MESH
BF = jnp.bfloat16
F32 = jnp.float32
PIECES = 12
LANES = 4
ROWS = 256
COLS = 128
VMEM_LIMIT = 62 * 2**20


def dot_nn(left, right):
    return lax.dot_general(left, right, (((1,), (0,)), ((), ())), preferred_element_type=F32)


def dot_nt(left, right):
    return lax.dot_general(left, right, (((1,), (1,)), ((), ())), preferred_element_type=F32)


def dot_tn(left, right):
    return lax.dot_general(left, right, (((0,), (0,)), ((), ())), preferred_element_type=F32)


class Place:
    def __init__(self, outer):
        dp = lax.axis_index("dp")
        self.z = lax.axis_index("mp")
        self.outer = outer
        self.own = lax.div(dp, outer)
        self.rest = lax.rem(dp, outer)
        self.core = lax.rem(self.own, 2)
        self.chip = lax.div(self.own, 2)
        col, row = lax.rem(self.chip, 2), lax.div(self.chip, 2)
        self.side = row * 2 + (1 - col)
        self.over = (1 - row) * 2 + col
        self.diag = (1 - row) * 2 + (1 - col)

    def dev(self, chip, core, z):
        return ((chip * 2 + core) * self.outer + self.rest, z)

    def partner(self):
        return self.dev(self.chip, 1 - self.core, self.z)

    def beside(self):
        return self.dev(self.side, self.core, self.z)

    def across(self):
        return self.dev(self.over, self.core, self.z)

    def along(self, k):
        return self.dev(self.chip, self.core, lax.rem(self.z + k, 4))


def greet(at):
    barrier = pltpu.get_barrier_semaphore()
    peers = [at.partner(), at.beside(), at.across()] + [at.along(k) for k in range(1, 4)]
    for peer in peers:
        pl.semaphore_signal(barrier, inc=1, device_id=peer, device_id_type=MESH)
    pl.semaphore_wait(barrier, len(peers))


def wait_for(ref, sem):
    pltpu.make_async_copy(ref, ref, sem).wait()


def send(src, dst, send_sem, recv_sem, device):
    pltpu.make_async_remote_copy(
        src, dst, send_sem, recv_sem, device_id=device, device_id_type=MESH
    ).start()


def when_in(piece, count, action):
    @pl.when(jnp.logical_and(piece >= 0, piece < count))
    def _():
        action(piece)


def cols_of(lane):
    return pl.ds(pl.multiple_of(lane * COLS, COLS), COLS)


def tile_rows(start, size):
    return pl.ds(pl.multiple_of(start, 128), size)


def gather_kernel(
    outer, shard, small, h, full, small_full, h_win,
    own_sem, sent, got_z, got_x, got_y, got_xd, got_yd, got_c, halo_sent, halo_got,
):
    at = Place(outer)
    greet(at)
    z, step = at.z, h.shape[0] // 5
    mine = [
        pltpu.make_async_copy(shard, full.at[:, z, :, cols_of(at.own)], own_sem.at[0]),
        pltpu.make_async_copy(small, small_full.at[pl.ds(z, 1), :, cols_of(at.own)], own_sem.at[1]),
        pltpu.make_async_copy(h, h_win.at[tile_rows(z * step, 5 * step)], own_sem.at[2]),
    ]
    x_lane, y_lane, d_lane = at.side * 2 + at.core, at.over * 2 + at.core, at.diag * 2 + at.core

    def source(p):
        return small if p is None else shard.at[pl.ds(p, 1)]

    def block(p, lane, start, count):
        ref = small_full if p is None else full.at[p]
        return ref.at[pl.ds(start, count), :, cols_of(lane)]

    def index(p):
        return PIECES if p is None else p

    def first(p):
        i, src, dst = index(p), source(p), block(p, at.own, z, 1)
        send(src, dst, sent.at[i], got_x.at[i], at.beside())
        send(src, dst, sent.at[i], got_y.at[i], at.across())
        for k in range(1, 4):
            send(src, dst, sent.at[i], got_z.at[i], at.along(k))
        send(src, dst, sent.at[i], got_c.at[i], at.partner())

    def second(p):
        i = index(p)
        wait_for(block(p, at.own, 0, 3), got_z.at[i])
        for k in range(1, 4):
            ref = block(p, at.own, lax.rem(z + k, 4), 1)
            send(ref, ref, sent.at[i], got_x.at[i], at.beside())
            send(ref, ref, sent.at[i], got_y.at[i], at.across())
            send(ref, ref, sent.at[i], got_c.at[i], at.partner())

    def third(p):
        i = index(p)
        wait_for(block(p, x_lane, 0, 4), got_x.at[i])
        ref = block(p, x_lane, 0, 2)
        send(ref, ref, sent.at[i], got_yd.at[i], at.across())
        ref = block(p, x_lane, 0, 4)
        send(ref, ref, sent.at[i], got_c.at[i], at.partner())
        wait_for(block(p, y_lane, 0, 4), got_y.at[i])
        ref = block(p, y_lane, 2, 2)
        send(ref, ref, sent.at[i], got_xd.at[i], at.beside())
        ref = block(p, y_lane, 0, 4)
        send(ref, ref, sent.at[i], got_c.at[i], at.partner())

    def fourth(p):
        i = index(p)
        wait_for(block(p, d_lane, 0, 2), got_yd.at[i])
        wait_for(block(p, d_lane, 2, 2), got_xd.at[i])
        ref = block(p, d_lane, 0, 4)
        send(ref, ref, sent.at[i], got_c.at[i], at.partner())

    def fifth(p):
        ref = small_full if p is None else full.at[p]
        wait_for(ref.at[:, :, 0 : 4 * COLS], got_c.at[index(p)])

    def drain(p):
        ref = small_full if p is None else full.at[p]
        wait_for(ref.at[:, :, 0 : 7 * COLS], sent.at[index(p)])
        wait_for(ref.at[0:3, :, 0:COLS], sent.at[index(p)])

    def halo():
        for i in range(3):
            @pl.when(jnp.logical_and(z >= 1, z < 4 - i))
            def _():
                dst = h_win.at[tile_rows((4 + z + i) * step, step)]
                send(h.at[tile_rows(i * step, step)], dst, halo_sent, halo_got, at.along(3))

            @pl.when(jnp.logical_and(z <= 2, z >= i))
            def _():
                dst = h_win.at[tile_rows(i * step, step)]
                send(h.at[tile_rows((4 - z + i) * step, step)], dst, halo_sent, halo_got, at.along(1))

    first(None)
    first(0)
    first(1)
    halo()
    for copy in mine:
        copy.start()
    stages = ((second, 0), (third, -1), (fourth, -2), (fifth, -3))

    def tick(t, carry):
        for action, shift in ((first, 2),) + stages:
            when_in(t + shift, PIECES, action)
        for action, shift in stages:
            @pl.when(t == -shift)
            def _():
                action(None)
        return carry

    lax.fori_loop(0, PIECES + 3, tick, 0)
    for copy in mine:
        copy.wait()
    wait_for(h_win.at[0 : 3 * step], halo_got)
    middle = jnp.logical_and(z >= 1, z <= 2)

    @pl.when(middle)
    def _():
        wait_for(h_win.at[0 : 5 * step], halo_sent)

    @pl.when(jnp.logical_not(middle))
    def _():
        wait_for(h_win.at[0:step], halo_sent)

    def drain_one(p, carry):
        drain(p)
        return carry

    lax.fori_loop(0, PIECES, drain_one, 0)
    drain(None)


def gather_weights(outer, shard, small, h):
    sem = pltpu.SemaphoreType.DMA
    step = h.shape[0] // 5
    return pl.pallas_call(
        functools.partial(gather_kernel, outer),
        out_shape=(
            jax.ShapeDtypeStruct((PIECES, 4, ROWS, 8 * COLS), BF),
            jax.ShapeDtypeStruct((4, 16, 8 * COLS), BF),
            jax.ShapeDtypeStruct((8 * step, h.shape[1]), BF),
        ),
        in_specs=[pl.BlockSpec(memory_space=pltpu.VMEM)] * 3,
        out_specs=[pl.BlockSpec(memory_space=pl.ANY)] * 3,
        scratch_shapes=[sem((3,))] + [sem((PIECES + 1,))] * 7 + [sem, sem],
        compiler_params=pltpu.CompilerParams(
            collective_id=1, has_side_effects=True, vmem_limit_bytes=VMEM_LIMIT
        ),
        name="gather",
    )(shard, small, h)


def scatter_kernel(
    outer, g_q, g_k, g_v, g_out, g_up, g_down, small, dh_win, out, small_out, halo_in,
    part, lane, got_c, got_dx, got_dy, got_x, got_y, got_z,
    s_part, s_lane, s_c, s_dx, s_dy, s_x, s_y, s_z,
    load_sem, sent0, sent1, sent2, sent3, sem_c, sem_dx, sem_dy, sem_x, sem_y, sem_z,
    halo_sent, halo_got, credit,
):
    at = Place(outer)
    greet(at)
    z, step = at.z, dh_win.shape[0] // 8
    singles = [(8, g_q), (9, g_k), (10, g_v), (11, g_out)]

    def load(p, action):
        slot = lax.rem(p, 2)

        def go(src):
            copy = pltpu.make_async_copy(src, part.at[slot], load_sem.at[slot])
            copy.start() if action == 0 else copy.wait()

        if action == 1:
            go(g_up.at[0])
            return

        @pl.when(p < 4)
        def _():
            go(g_down.at[p])

        @pl.when(jnp.logical_and(p >= 4, p < 8))
        def _():
            go(g_up.at[lax.rem(p, 4)])

        for i, ref in singles:
            @pl.when(p == i)
            def _():
                go(ref)

    def first(p):
        slot = lax.rem(p, 2)
        load(p, 1)

        @pl.when(p >= 2)
        def _():
            pl.semaphore_wait(credit, 1)

        for a in range(4):
            src = part.at[slot, :, :, cols_of(a * 2 + 1 - at.core)]
            send(src, got_c.at[slot, a], sent0.at[p], sem_c.at[p], at.partner())

    def second(p):
        slot, row = lax.rem(p, 2), lax.rem(p, LANES)
        wait_for(got_c.at[slot], sem_c.at[p])

        @pl.when(p >= LANES)
        def _():
            wait_for(lane.at[row, 0], sent1.at[p - LANES])
            wait_for(lane.at[row, 0:2], sent2.at[p - LANES])
            wait_for(lane.at[row, 0, 0:3], sent3.at[p - LANES])

        def add(i, carry):
            a, b = lax.div(i, 4), lax.rem(i, 4)
            lane[row, a, b] = part[slot, b, :, cols_of(a * 2 + at.core)] + got_c[slot, a, b]
            return carry

        lax.fori_loop(0, 16, add, 0)

        @pl.when(p < PIECES - 2)
        def _():
            pl.semaphore_signal(credit, inc=1, device_id=at.partner(), device_id_type=MESH)

        wait_for(got_c.at[slot], sent0.at[p])

        @pl.when(p + 2 < PIECES)
        def _():
            load(p + 2, 0)

        send(lane.at[row, at.diag, 0:2], got_dy.at[p], sent1.at[p], sem_dy.at[p], at.across())
        send(lane.at[row, at.diag, 2:4], got_dx.at[p], sent1.at[p], sem_dx.at[p], at.beside())

    def third(p):
        row = lax.rem(p, LANES)
        wait_for(got_dy.at[p], sem_dy.at[p])

        def add_y(i, carry):
            lane[row, at.side, i] = lane[row, at.side, i] + got_dy[p, i]
            return carry

        lax.fori_loop(0, 2, add_y, 0)
        send(lane.at[row, at.side], got_x.at[p], sent2.at[p], sem_x.at[p], at.beside())
        wait_for(got_dx.at[p], sem_dx.at[p])

        def add_x(i, carry):
            lane[row, at.over, i + 2] = lane[row, at.over, i + 2] + got_dx[p, i]
            return carry

        lax.fori_loop(0, 2, add_x, 0)
        send(lane.at[row, at.over], got_y.at[p], sent2.at[p], sem_y.at[p], at.across())

    def fourth(p):
        row = lax.rem(p, LANES)
        wait_for(got_x.at[p], sem_x.at[p])
        wait_for(got_y.at[p], sem_y.at[p])

        def add(i, carry):
            total = lane[row, at.chip, i].astype(F32) + got_x[p, i].astype(F32)
            lane[row, at.chip, i] = (total + got_y[p, i].astype(F32)).astype(BF)
            return carry

        lax.fori_loop(0, 4, add, 0)
        for k in range(1, 4):
            block = lane.at[row, at.chip, lax.rem(z + k, 4)]
            send(block, got_z.at[p, k - 1], sent3.at[p], sem_z.at[p], at.along(k))

    def fifth(p):
        row = lax.rem(p, LANES)
        wait_for(got_z.at[p], sem_z.at[p])
        total = lane[row, at.chip, z].astype(F32)
        for k in range(3):
            total = total + got_z[p, k].astype(F32)
        out[p] = total

    n = PIECES

    def small_first():
        pltpu.make_async_copy(small, s_part, load_sem.at[2]).wait()
        for a in range(4):
            src = s_part.at[:, :, cols_of(a * 2 + 1 - at.core)]
            send(src, s_c.at[a], sent0.at[n], sem_c.at[n], at.partner())

    def small_second():
        wait_for(s_c, sem_c.at[n])
        for a in range(4):
            s_lane[a] = s_part[:, :, cols_of(a * 2 + at.core)] + s_c[a]
        send(s_lane.at[at.diag, 0:2], s_dy, sent1.at[n], sem_dy.at[n], at.across())
        send(s_lane.at[at.diag, 2:4], s_dx, sent1.at[n], sem_dx.at[n], at.beside())

    def small_third():
        wait_for(s_dy, sem_dy.at[n])
        s_lane[at.side, 0:2] = s_lane[at.side, 0:2] + s_dy[...]
        send(s_lane.at[at.side], s_x, sent2.at[n], sem_x.at[n], at.beside())
        wait_for(s_dx, sem_dx.at[n])
        s_lane[at.over, 2:4] = s_lane[at.over, 2:4] + s_dx[...]
        send(s_lane.at[at.over], s_y, sent2.at[n], sem_y.at[n], at.across())

    def small_fourth():
        wait_for(s_x, sem_x.at[n])
        wait_for(s_y, sem_y.at[n])
        s_lane[at.chip] = s_lane[at.chip] + s_x[...] + s_y[...]
        for k in range(1, 4):
            block = s_lane.at[at.chip, lax.rem(z + k, 4)]
            send(block, s_z.at[k - 1], sent3.at[n], sem_z.at[n], at.along(k))

    def small_fifth():
        wait_for(s_z, sem_z.at[n])
        small_out[...] = s_lane[at.chip, z] + s_z[0] + s_z[1] + s_z[2]

    def halo():
        for i in range(3):
            @pl.when(z > i)
            def _():
                src = dh_win.at[tile_rows(i * step, step)]
                dst = halo_in.at[tile_rows((5 - z + i) * step, step)]
                send(src, dst, halo_sent, halo_got, at.along(3))

            @pl.when(z < 3 - i)
            def _():
                src = dh_win.at[tile_rows((5 + z + i) * step, step)]
                dst = halo_in.at[tile_rows(i * step, step)]
                send(src, dst, halo_sent, halo_got, at.along(1))

    pltpu.make_async_copy(small, s_part, load_sem.at[2]).start()
    load(0, 0)
    load(1, 0)
    halo()
    stages = ((first, 0), (second, -1), (third, -2), (fourth, -3), (fifth, -4))
    small_stages = (small_first, small_second, small_third, small_fourth, small_fifth)

    def tick(t, carry):
        for action, shift in stages:
            when_in(t + shift, PIECES, action)
        for i, action in enumerate(small_stages):
            @pl.when(t == i + 1)
            def _():
                action()
        return carry

    lax.fori_loop(0, PIECES + 4, tick, 0)
    for p in range(PIECES - LANES, PIECES):
        row = p % LANES
        wait_for(lane.at[row, 0], sent1.at[p])
        wait_for(lane.at[row, 0:2], sent2.at[p])
        wait_for(lane.at[row, 0, 0:3], sent3.at[p])
    wait_for(s_c, sent0.at[n])
    wait_for(s_lane.at[0], sent1.at[n])
    wait_for(s_lane.at[0:2], sent2.at[n])
    wait_for(s_lane.at[0, 0:3], sent3.at[n])
    wait_for(dh_win.at[0 : 3 * step], halo_sent)
    middle = jnp.logical_and(z >= 1, z <= 2)

    @pl.when(middle)
    def _():
        wait_for(halo_in.at[0 : 5 * step], halo_got)

    @pl.when(jnp.logical_not(middle))
    def _():
        wait_for(halo_in.at[0:step], halo_got)


def scatter_grads(outer, grads, small, dh_win):
    sem = pltpu.SemaphoreType.DMA
    half = (4, 4, ROWS, COLS)
    step = dh_win.shape[0] // 8
    anywhere, vmem = pl.BlockSpec(memory_space=pl.ANY), pl.BlockSpec(memory_space=pltpu.VMEM)
    return pl.pallas_call(
        functools.partial(scatter_kernel, outer),
        out_shape=(
            jax.ShapeDtypeStruct((PIECES, ROWS, COLS), F32),
            jax.ShapeDtypeStruct((8, COLS), F32),
            jax.ShapeDtypeStruct((5 * step, dh_win.shape[1]), BF),
        ),
        in_specs=[anywhere] * 8,
        out_specs=[vmem, vmem, anywhere],
        scratch_shapes=[
            pltpu.VMEM((2, 4, ROWS, 8 * COLS), BF),
            pltpu.VMEM((LANES,) + half, BF),
            pltpu.VMEM((2,) + half, BF),
            pltpu.VMEM((PIECES, 2, ROWS, COLS), BF),
            pltpu.VMEM((PIECES, 2, ROWS, COLS), BF),
            pltpu.VMEM((PIECES, 4, ROWS, COLS), BF),
            pltpu.VMEM((PIECES, 4, ROWS, COLS), BF),
            pltpu.VMEM((PIECES, 3, ROWS, COLS), BF),
            pltpu.VMEM((4, 8, 8 * COLS), F32),
            pltpu.VMEM((4, 4, 8, COLS), F32),
            pltpu.VMEM((4, 4, 8, COLS), F32),
            pltpu.VMEM((2, 8, COLS), F32),
            pltpu.VMEM((2, 8, COLS), F32),
            pltpu.VMEM((4, 8, COLS), F32),
            pltpu.VMEM((4, 8, COLS), F32),
            pltpu.VMEM((3, 8, COLS), F32),
            sem((3,)),
        ]
        + [sem((PIECES + 1,))] * 10
        + [sem, sem, pltpu.SemaphoreType.REGULAR],
        compiler_params=pltpu.CompilerParams(
            collective_id=2, has_side_effects=True, vmem_limit_bytes=VMEM_LIMIT
        ),
        name="scatter",
    )(*grads, small, dh_win)


def split_heads(rows):
    low = lax.broadcasted_iota(jnp.int32, rows.shape, 1) < rows.shape[1] // 2
    zero = jnp.zeros_like(rows)
    return jnp.concatenate([jnp.where(low, rows, zero), jnp.where(low, zero, rows)], axis=0)


def join_heads(both):
    half = both.shape[1] // 2
    low = lax.broadcasted_iota(jnp.int32, (both.shape[0], half), 0) < both.shape[0] // 2
    return jnp.where(low, both[:, :half], both[:, half:]).T


def masked_scores(keys, q_two, live):
    scores = dot_nt(keys, q_two)
    return jnp.where(lax.broadcasted_iota(jnp.int32, scores.shape, 0) < live, scores, MASKED)


def attend_kernel(scale, meta, q_ref, k_ref, v_ref, o_ref, lse_ref, v_t):
    seq_len, step = k_ref.shape[0] // 2, q_ref.shape[0] // 5
    v_t[...] = v_ref[...].T
    for j in range(5):
        slot = meta[j]
        keys = tile_rows(slot * seq_len, seq_len)
        rows = slice(j * step, (j + 1) * step)
        q_two = split_heads(q_ref[rows, :] * jnp.asarray(scale, BF))
        scores = masked_scores(k_ref[keys, :], q_two, meta[5 + slot])
        row_max = jnp.max(scores, axis=0, keepdims=True)
        expo = jnp.exp(scores - row_max)
        total = jnp.sum(expo, axis=0, keepdims=True)
        mixed = dot_nn(v_t[:, keys], expo.astype(BF)) / total
        o_ref[rows, :] = join_heads(mixed).astype(BF)
        lse_ref[0, j : j + 1, :] = row_max + jnp.log(total)


def attend(meta, q, k, v, head):
    rows, model = q.shape
    win, step, wide = k.shape[0], rows // 5, 2 * head
    block = lambda n: pl.BlockSpec((n, wide), lambda i, m: (0, i))
    return pl.pallas_call(
        functools.partial(attend_kernel, head**-0.5),
        out_shape=(
            jax.ShapeDtypeStruct((rows, model), BF),
            jax.ShapeDtypeStruct((model // wide, 8, 2 * step), F32),
        ),
        grid_spec=pltpu.PrefetchScalarGridSpec(
            num_scalar_prefetch=1,
            grid=(model // wide,),
            in_specs=[block(rows), block(win), block(win)],
            out_specs=[block(rows), pl.BlockSpec((1, 8, 2 * step), lambda i, m: (i, 0, 0))],
            scratch_shapes=[pltpu.VMEM((wide, win), BF)],
        ),
        compiler_params=pltpu.CompilerParams(vmem_limit_bytes=VMEM_LIMIT // 2),
        name="attend",
    )(meta, q, k, v)


def attend_back_kernel(
    scale, meta, q_ref, k_ref, v_ref, g_ref, lse_ref, dq_ref, dk_ref, dv_ref, k_t, dk_acc, dv_acc
):
    seq_len, step = k_ref.shape[0] // 2, q_ref.shape[0] // 5
    k_t[...] = k_ref[...].T
    dk_acc[...] = jnp.zeros_like(dk_acc)
    dv_acc[...] = jnp.zeros_like(dv_acc)
    for j in range(5):
        slot = meta[j]
        keys = tile_rows(slot * seq_len, seq_len)
        rows = slice(j * step, (j + 1) * step)
        q_two = split_heads(q_ref[rows, :] * jnp.asarray(scale, BF))
        g_two = split_heads(g_ref[rows, :])
        scores = masked_scores(k_ref[keys, :], q_two, meta[5 + slot])
        probs = jnp.exp(scores - lse_ref[0, j : j + 1, :])
        dv_acc[keys, :] += dot_nn(probs.astype(BF), g_two)
        grad_p = dot_nt(v_ref[keys, :], g_two)
        inner = jnp.sum(probs * grad_p, axis=0, keepdims=True)
        grad_s = (probs * (grad_p - inner)).astype(BF)
        dk_acc[keys, :] += dot_nn(grad_s, q_two)
        dq_ref[rows, :] = (join_heads(dot_nn(k_t[:, keys], grad_s)) * scale).astype(BF)
    dk_ref[...] = dk_acc[...].astype(BF)
    dv_ref[...] = dv_acc[...].astype(BF)


def attend_back(meta, q, k, v, g, lse, head):
    rows, model = q.shape
    win, step, wide = k.shape[0], rows // 5, 2 * head
    block = lambda n: pl.BlockSpec((n, wide), lambda i, m: (0, i))
    return pl.pallas_call(
        functools.partial(attend_back_kernel, head**-0.5),
        out_shape=(
            jax.ShapeDtypeStruct((rows, model), BF),
            jax.ShapeDtypeStruct((win, model), BF),
            jax.ShapeDtypeStruct((win, model), BF),
        ),
        grid_spec=pltpu.PrefetchScalarGridSpec(
            num_scalar_prefetch=1,
            grid=(model // wide,),
            in_specs=[
                block(rows), block(win), block(win), block(rows),
                pl.BlockSpec((1, 8, 2 * step), lambda i, m: (i, 0, 0)),
            ],
            out_specs=[block(rows), block(win), block(win)],
            scratch_shapes=[
                pltpu.VMEM((wide, win), BF), pltpu.VMEM((win, wide), F32), pltpu.VMEM((win, wide), F32)
            ],
        ),
        compiler_params=pltpu.CompilerParams(vmem_limit_bytes=VMEM_LIMIT // 2),
        name="attend_back",
    )(meta, q, k, v, g, lse)


def layer_norm(values_in, gain, shift):
    average = jnp.mean(values_in, axis=-1, keepdims=True)
    centred = values_in - average
    variance = jnp.mean(centred * centred, axis=-1, keepdims=True)
    return centred * lax.rsqrt(variance + LN_EPS) * gain + shift


def gelu_exact(values_in):
    return jax.nn.gelu(values_in, approximate=False)


def body(
    outer, tokens, context, timestep, time_weight, time_bias, qkv_weight, qv_bias, out_weight, out_bias,
    gain_one, shift_one, up_weight, up_bias, down_weight, down_bias, gain_two, shift_two, cotangent,
):
    z = lax.axis_index("mp")
    rows, model = tokens.shape
    seqs = context.shape[0]
    seq_len = rows * 4 // seqs
    step = rows // 5
    groups = None
    if outer > 1:
        groups = [[i * outer + j for j in range(outer)] for i in range(8)]
        qkv_weight, out_weight, up_weight, down_weight, qv_bias, up_bias = (
            lax.all_gather(w, "dp", axis=1, tiled=True, axis_index_groups=groups)
            for w in (qkv_weight, out_weight, up_weight, down_weight, qv_bias, up_bias)
        )
    shard = jnp.concatenate(
        [
            qkv_weight.transpose(0, 2, 1),
            out_weight.reshape(1, ROWS, COLS),
            up_weight.reshape(4, ROWS, COLS),
            down_weight.reshape(4, ROWS, COLS),
        ]
    )
    flat = jnp.concatenate([up_bias.reshape(-1), qv_bias.reshape(-1)])
    n_up, n_qv = up_bias.size, qv_bias.size
    small = jnp.pad(flat, (0, 16 * COLS - flat.size)).reshape(1, 16, COLS)
    row_ids = z * rows + jnp.arange(rows, dtype=jnp.int32)
    owner = (row_ids // seq_len)[:, None] == jnp.arange(seqs, dtype=jnp.int32)[None, :]
    portion = timestep.astype(F32) / TSTEPS
    fraction = jnp.sum(jnp.where(owner, portion[None, :], 0.0), axis=1)
    h_zero = tokens.astype(F32) + fraction[:, None] * time_weight + time_bias
    h_low = h_zero.astype(BF)
    full, small_full, h_win = gather_weights(outer, shard, small, h_low)
    w_q, w_k, w_v, w_out = (full[i].reshape(model, model) for i in range(4))
    w_up, w_down = full[4:8].reshape(4 * model, model), full[8:12].reshape(4 * model, model)
    flat = small_full.reshape(4, 16, 8, COLS)[:, :2].transpose(0, 2, 1, 3).reshape(4, 8, 2 * COLS)
    up_all = flat[:, :, :n_up].reshape(4, 8, 4, 2, 16).transpose(2, 0, 3, 1, 4).reshape(-1)
    qv_all = flat[:, :, n_up : n_up + n_qv].reshape(4, 8, 4, 16).transpose(0, 2, 1, 3).reshape(16, 2, -1)
    heads, head = qv_all.shape[0], qv_all.shape[2]
    bias_f = qv_all.astype(F32)
    queries = (dot_nt(h_low, w_q) + bias_f[:, 0].reshape(-1)).astype(BF)
    keys = dot_nt(h_win, w_k).astype(BF)
    values = (dot_nt(h_win, w_v) + bias_f[:, 1].reshape(-1)).astype(BF)
    live = (context + BLOCK).astype(jnp.int32)
    slots = (z + jnp.arange(5, dtype=jnp.int32)) // 4
    meta = jnp.concatenate([slots, lax.dynamic_slice(live, (z,), (2,))])
    attn, lse = attend(meta, queries, keys, values, head)
    branch_a = dot_nn(attn, w_out) + out_bias
    y_one, ln_one_back = jax.vjp(layer_norm, h_zero + branch_a, gain_one, shift_one)
    y_low = y_one.astype(BF)
    pre = dot_nt(y_low, w_up) + up_all.astype(F32)
    hidden, gelu_back = jax.vjp(gelu_exact, pre)
    hidden_low = hidden.astype(BF)
    branch_f = dot_nn(hidden_low, w_down) + down_bias
    y_two, ln_two_back = jax.vjp(layer_norm, y_one + branch_f, gain_two, shift_two)
    layer_out = y_two.astype(BF)
    grad_z2, grad_gain_two, grad_shift_two = ln_two_back(cotangent.astype(F32))
    grad_f = grad_z2.astype(BF)
    grad_down_bias = jnp.sum(grad_f.astype(F32), axis=0)
    (grad_pre,) = gelu_back(dot_nt(grad_f, w_down))
    grad_pre = grad_pre.astype(BF)
    grad_up = dot_tn(grad_pre, y_low).astype(BF)
    grad_down = dot_tn(hidden_low, grad_f).astype(BF)
    grad_up_bias = jnp.sum(grad_pre.astype(F32), axis=0)
    grad_y1 = grad_z2 + dot_nn(grad_pre, w_up)
    grad_z1, grad_gain_one, grad_shift_one = ln_one_back(grad_y1)
    grad_a = grad_z1.astype(BF)
    grad_out_bias = jnp.sum(grad_a.astype(F32), axis=0)
    grad_attn = dot_nt(grad_a, w_out).astype(BF)
    grad_out_w = dot_tn(attn, grad_a).astype(BF)
    dq, dk, dv = attend_back(meta, queries, keys, values, grad_attn, lse, head)
    grad_qv_bias = jnp.stack(
        [
            jnp.sum(dq.astype(F32), axis=0).reshape(heads, head),
            jnp.sum(dv.astype(F32), axis=0).reshape(heads, head),
        ],
        axis=1,
    )
    dh_win = dot_nn(dk, w_k) + dot_nn(dv, w_v)
    dh_own = grad_z1 + dot_nn(dq, w_q)
    portion_two = jnp.repeat(lax.dynamic_slice(portion, (z,), (2,)), seq_len)
    grad_time_weight = jnp.sum(fraction[:, None] * dh_own, axis=0) + jnp.sum(
        portion_two[:, None] * dh_win, axis=0
    )
    grad_time_bias = jnp.sum(dh_own, axis=0) + jnp.sum(dh_win, axis=0)
    dh_own = dh_own + lax.dynamic_slice(dh_win, (z * step, 0), (rows, model))
    spread = model // (32 * outer)
    vectors = jnp.stack(
        [
            grad_time_weight, grad_time_bias, grad_out_bias, grad_gain_one, grad_shift_one,
            grad_down_bias, grad_gain_two, grad_shift_two,
        ]
    )
    packed = jnp.concatenate(
        [
            vectors.reshape(8, 8, outer, 4, spread).transpose(3, 1, 0, 2, 4).reshape(4, 8, -1),
            grad_up_bias.reshape(4, 4, 2, 8, 16).transpose(1, 3, 0, 2, 4).reshape(4, 8, -1),
            grad_qv_bias.reshape(4, 4, 8, 16).transpose(0, 2, 1, 3).reshape(4, 8, -1),
        ],
        axis=2,
    )
    n_vec = 8 * outer * spread
    packed = jnp.pad(packed, ((0, 0), (0, 0), (0, 8 * COLS - packed.shape[2])))
    packed = packed.reshape(4, 8, 8, COLS).transpose(0, 2, 1, 3).reshape(4, 8, 8 * COLS)
    square = (4, ROWS, model)
    tall = (4,) + square
    grads = (
        dot_tn(dq, h_low).astype(BF).reshape(square),
        dot_tn(dk, h_win).astype(BF).reshape(square),
        dot_tn(dv, h_win).astype(BF).reshape(square),
        grad_out_w.reshape(square),
        grad_up.reshape(tall),
        grad_down.reshape(tall),
    )
    done, small_done, halo_in = scatter_grads(outer, grads, packed, dh_win.astype(BF))
    local = jnp.arange(rows, dtype=jnp.int32)
    edge = (4 - z) * step
    reached = jnp.logical_or(
        jnp.logical_and(z <= 2, local >= edge), jnp.logical_and(z >= 1, local < edge)
    )
    grad_tokens = dh_own + jnp.where(reached[:, None], halo_in.astype(F32), 0.0)
    small_done = small_done.reshape(-1)
    results = [
        done[8:11].transpose(0, 2, 1),
        done[11],
        done[4:8].reshape(4 * ROWS, COLS),
        done[0:4].reshape(4 * ROWS, COLS),
        small_done[n_vec : n_vec + n_up].reshape(8, 16),
        small_done[n_vec + n_up : n_vec + n_up + n_qv].reshape(4, 16),
        small_done[:n_vec].reshape(8, outer * spread),
    ]
    if outer > 1:
        results = [
            lax.psum_scatter(g, "dp", scatter_dimension=1, tiled=True, axis_index_groups=groups)
            for g in results
        ]
    grad_qkv, grad_out_w, grad_up, grad_down, grad_up_bias, grad_qv_bias, vectors = results
    return (
        layer_out, grad_tokens, vectors[0], vectors[1], grad_qkv, grad_qv_bias,
        grad_out_w, vectors[2], vectors[3], vectors[4], grad_up, grad_up_bias,
        grad_down, vectors[5], vectors[6], vectors[7],
    )


def solution(mesh):
    outer = mesh.shape["dp"] // 8
    placed = (
        P(("dp", "mp"), None), P("dp"), P("dp"), P(), P(), P(None, "dp", "mp"), P("mp", "dp"), P("mp", "dp"),
        P(), P(), P(), P("mp", "dp"), P("mp", "dp"), P("mp", "dp"), P(), P(), P(), P(("dp", "mp"), None),
    )
    spread = P(("dp", "mp"))
    wide = P("mp", "dp")
    return jax.shard_map(
        functools.partial(body, outer),
        mesh=mesh,
        in_specs=placed,
        out_specs=(
            P(("dp", "mp"), None), P(("dp", "mp"), None), spread, spread, P(None, "dp", "mp"), wide, wide,
            spread, spread, spread, wide, wide, wide, spread, spread, spread,
        ),
        check_vma=False,
    )
```

time: 907 us -> 505 us (0.56)
  local copies, waits for them, and re-layouts: 209 us -> 39.6 us
  blocking collectives: 83.5 us -> 0 us
  matrix products: 206 us -> 136 us
  other arithmetic: 68.6 us -> 19.6 us
  loops' own time: 39.5 us -> 0 us
  Pallas kernels: 278 us -> 299 us
  between operations: 15.2 us -> 1.85 us
    dot_general x41 -> x6, matrix products: 110 us -> 36.8 us  [dot_nn(): lax.dot_general(left, right, (((1,), (0,)), ((), ())), preferred_element_...]
    all_gather x4 -> x0, blocking collectives: 43.2 us -> none  [the longest x1 12.9 us: body(): lax.all_gather(lax.all_gather(qv_bias, 'dp', axis=1, tiled=True), 'mp', a...]
    transpose x5 -> x4, local copies, waits for them, and re-layouts: 43.8 us -> 0.85 us  [the longest x1 0.72 us: body(): grad_up_bias.reshape(4, 4, 2, 8, 16).transpose(1, 3, 0, 2, 4)]
    unnamed x1 -> x0, blocking collectives: 40.3 us -> none
    another operation x2 -> x0, loops' own time: 39.5 us -> none  [the longest x1 19.9 us: body(): (dk, dv), dq = lax.scan(back, (zero, zero), jnp.arange(5))]
    reshape x10 -> x11, local copies, waits for them, and re-layouts: 44.4 us -> 5.14 us  [the longest x2 1.89 us: body(): grad_up_bias.reshape(4, 4, 2, 8, 16).transpose(1, 3, 0, 2, 4)]
    unnamed x150 -> x118, local copies, waits for them, and re-layouts: 40.4 us -> 11.2 us
    while x46 -> x0, local copies, waits for them, and re-layouts: 24.8 us -> none  [the longest x4 16.1 us: body(): lax.map(lambda j: attend(record_of(j)), jnp.arange(5)).reshape(rows, model)]
  transfers between devices with their start and end apart: 2 -> 0, of which waited for: 0 -> 0; matrix products, arithmetic and copies ran while one was open for 20% -> 0% of each run, Pallas kernels for 31% -> 0%
where the time goes in v2:
time: 505 us; the launch traced here: 496 us
  Pallas kernels  299 us (59%)
  matrix products  136 us (27%)
  local copies, waits for them, and re-layouts  39.6 us (8%)
  other arithmetic  19.6 us (4%)
    pallas_call x1, Pallas kernels, gather_weights(): pl.pallas_call(functools.partial(gather_kernel, outer), out_shape=(jax.Sh...  129 us
    pallas_call x1, Pallas kernels, scatter_grads(): pl.pallas_call(functools.partial(scatter_kernel, outer), out_shape=(jax.S...  121 us
    dot_general x6, matrix products, dot_nt(): lax.dot_general(left, right, (((1,), (1,)), ((), ())), preferred_element_...  66.5 us
    dot_general x6, matrix products, dot_nn(): lax.dot_general(left, right, (((1,), (0,)), ((), ())), preferred_element_...  36.8 us
    dot_general x6, matrix products, dot_tn(): lax.dot_general(left, right, (((0,), (0,)), ((), ())), preferred_element_...  32.9 us
    pallas_call x1, Pallas kernels, attend_back(): pl.pallas_call(functools.partial(attend_back_kernel, head ** (-0.5)), out...  29.4 us
    pallas_call x1, Pallas kernels, attend(): pl.pallas_call(functools.partial(attend_kernel, head ** (-0.5)), out_shap...  20.3 us
    slice x1, local copies, waits for them, and re-layouts, body(): full[8:12].reshape(4 * model, model)  11.6 us

profile of v2, /device:TPU:0, one launch (start us, length us, event | category | flops | bytes accessed | tf_op | source)
XLA Modules:
  0.0 496.1 jit_solution(2516544297564326542)
XLA Ops:
  0.7 1.2 copy.46
  1.8 2.0 pad_maximum_fusion.shard
  3.9 0.8 reshape.298
  4.6 0.8 reshape.297
  5.4 0.6 fusion.17.small
  6.0 0.7 convert_multiply_fusion.2
  6.7 0.4 copy-done.39
  7.2 2.2 fusion.10.h
  9.4 128.6 %gather.1 = (bf16[12,4,256,1024]{3,2,1,0:T(8,128)(2,1)}, bf16[4,16,1024]{2,1,0:T(8,128)(2,1)}, bf16[1024,1024]{1,0:T(8,128)(2,1)}) custom-call(bf16[12,256,128]{2,1,0:T(8,128)(2,1)} %pad_maximum_fusion.shard, bf16[1,16,128]{2,1,0:T(8,128)(2,1)} %fusion.17.small, bf16[640,1024]{1,0:T(8,128)(2,1)} %fusion.10.h), custom_call_target="tpu_custom_call" | custom-call | tf_op jit(solution)/shard_map/gather/pallas_call | solution.py:222
  138.0 0.9 copy.54
  139.0 0.2 reshape.324
  139.2 0.1 reshape.322
  139.4 11.6 %fusion.33 = (bf16[4,4,256,1024]{3,2,1,0:T(8,128)(2,1)}, bf16[4,4,256,1024]{3,2,1,0:T(8,128)(2,1)}) fusion(bf16[12,4,256,1024]{3,2,1,0:T(8,128)(2,1)} %get-tuple-element.27), kind=kLoop, calls=%fused_computation.135 | loop fusion | bytes 33554432 | tf_op jit(solution)/shard_map/slice | solution.py:643
  151.2 6.1 %fusion.34 = (bf16[1,4,256,1024]{3,2,1,0:T(8,128)(2,1)}, bf16[1,4,256,1024]{3,2,1,0:T(8,128)(2,1)}, bf16[1,4,256,1024]{3,2,1,0:T(8,128)(2,1)}, bf16[1,4,256,1024]{3,2,1,0:T(8,128)(2,1)}) fusion(bf16[12,4,256,1024]{3,2,1,0:T(8,128)(2,1)} %get-tuple-element.27), kind=kLoop, calls=%fused_computation.136 | loop fusion | bytes 16777216 | tf_op jit(solution)/shard_map/slice | solution.py:642
  157.3 0.1 reshape.323
  157.7 3.3 add_convert_fusion.3.q_ref
  161.0 2.4 convolution_convert_fusion.4.k_ref
  163.5 4.6 add_convert_fusion.1.v_ref
  168.1 20.3 %attend.1 = (bf16[640,1024]{1,0:T(8,128)(2,1)S(1)}, f32[8,8,256]{2,1,0:T(8,128)S(1)}) custom-call(s32[7]{0:T(128)S(1)} %pad_add_fusion.meta, bf16[640,1024]{1,0:T(8,128)(2,1)S(1)} %add_convert_fusion.3.q_ref, bf16[1024,1024]{1,0:T(8,128)(2,1)S(1)} %convolution_convert_fusion.4.k_ref, bf16[1024,1024]{1,0:T(8,128)(2,1)S(1)} %add_convert_fusion.1.v_ref), custom_call_target="tpu_custom_call" | custom-call | tf_op jit(solution)/shard_map/attend/pallas_call | solution.py:526
  188.6 1.8 fusion.36
  190.4 0.4 multiply_reduce_fusion.5
  190.8 0.3 slice-done
  191.2 2.2 slice-done.1
  193.4 36.3 %multiply_convert_fusion = (bf16[640,4096]{1,0:T(8,128)(2,1)}, f32[640,4096]{1,0:T(8,128)}, f32[640,4096]{1,0:T(8,128)}) fusion(f32[4096]{0:T(1024)S(1)} %reshape.322, bf16[4096,1024]{1,0:T(8,128)(2,1)S(1)} %bitcast.110, f32[640,1024]{1,0:T(8,128)S(1)} %get-tuple-element.145, f32[1024]{0:T(1024)S(1)} %copy-done.45, f32[1024]{0:T(1024)S(1)} %copy-done.33, ...), kind=kOutput, calls=%fused_computation.4 | convolution fusion | flops 5545000960 | bytes 37254144 | tf_op jit(solution)/shard_map/dot_general | solution.py:29
  229.7 10.4 %fusion.37 = (f32[640]{0:T(1024)S(1)}, f32[640,1024]{1,0:T(8,128)S(1)}) fusion(f32[1024]{0:T(1024)S(1)} %copy-done.44, bf16[640,4096]{1,0:T(8,128)(2,1)} %get-tuple-element.124, bf16[4096,1024]{1,0:T(8,128)(2,1)} %bitcast.111, f32[1024]{0:T(1024)S(1)} %copy-done.45, f32[1024]{0:T(1024)S(1)} %copy-done.33, f32[640]{0:T(1024)S(1)} %fusion.23, ...), kind=kOutput, calls=%fused_computation.139 | convolution fusion | flops 5373296128 | bytes 18894336 | tf_op jit(solution)/shard_map/dot_general | solution.py:25
  240.1 0.4 multiply_reduce_fusion.4
  240.5 0.9 copy-done.14
  241.4 1.6 fusion.9
  243.0 2.2 fusion.31
  245.1 1.5 copy-done.11
  246.7 2.0 convert_reduce_fusion.4
  248.6 18.3 %convert_reduce_fusion = (f32[4096]{0:T(1024)}, bf16[640,4096]{1,0:T(8,128)(2,1)}) fusion(f32[640,4096]{1,0:T(8,128)} %get-tuple-element.125, f32[640,4096]{1,0:T(8,128)} %get-tuple-element.146, f32[4096]{0:T(1024)S(1)} %reshape.322, bf16[640,1024]{1,0:T(8,128)(2,1)} %get-tuple-element.115, bf16[4096,1024]{1,0:T(8,128)(2,1)} %bitcast.112), kind=kOutput, calls=%fused_computation.2 | convolution fusion | flops 5413269504 | bytes 35946496 | tf_op jit(solution)/shard_map/dot_general | solution.py:29
  266.9 12.2 %multiply_reduce_fusion.1 = (f32[1024]{0:T(1024)}, f32[640]{0:T(1024)S(1)}, f32[1024]{0:T(1024)}, f32[640,1024]{1,0:T(8,128)S(1)}) fusion(f32[640,1024]{1,0:T(8,128)} %copy-done.8, f32[640]{0:T(1024)S(1)} %fusion.23, f32[640]{0:T(1024)S(1)} %broadcast_multiply_fusion.1, f32[1024]{0:T(1024)S(1)} %copy-done.33, bf16[640,4096]{1,0:T(8,128)(2,1)} %get-tuple-element.119, ...), kind=kOutput, calls=%fused_computation.35 | convolution fusion | flops 5375260160 | bytes 21518336 | tf_op jit(solution)/shard_map/dot_general | solution.py:25
  279.1 0.9 fusion.30
  280.0 0.9 convert_reduce_fusion.5
  280.9 1.6 copy-done.20
  282.5 1.6 convolution_convert_fusion.7.g_ref
  284.1 29.4 %attend_back.1 = (bf16[640,1024]{1,0:T(8,128)(2,1)S(1)}, bf16[1024,1024]{1,0:T(8,128)(2,1)S(1)}, bf16[1024,1024]{1,0:T(8,128)(2,1)S(1)}) custom-call(s32[7]{0:T(128)S(1)} %pad_add_fusion.meta, bf16[640,1024]{1,0:T(8,128)(2,1)S(1)} %add_convert_fusion.3.q_ref, bf16[1024,1024]{1,0:T(8,128)(2,1)S(1)} %convolution_convert_fusion.4.k_ref, ...), custom_call_target="tpu_custom_call" | custom-call | tf_op jit(solution)/shard_map/attend_back/pallas_call | solution.py:573
  313.6 3.2 convolution_convert_fusion.6
  316.7 3.7 convolution_convert_fusion.3
  320.5 3.8 convolution_convert_fusion.2
  324.3 3.2 convolution_convert_fusion.5
  327.5 9.8 %convolution_convert_fusion.1 = bf16[4096,1024]{1,0:T(8,128)(2,1)} fusion(bf16[640,4096]{1,0:T(8,128)(2,1)S(1)} %bitcast.143, f32[640,1024]{1,0:T(8,128)S(1)} %copy-done.9, f32[1024]{0:T(1024)S(1)} %copy-done.45, f32[1024]{0:T(1024)S(1)} %copy-done.33, f32[640]{0:T(1024)S(1)} %fusion.23, f32[640]{0:T(1024)S(1)} %broadcast_multiply_fusion.1), kind=kOutput, calls=%fused_computation.19 | convolution fusion | flops 5376180224 | bytes 16266240 | tf_op jit(solution)/shard_map/dot_general | solution.py:33
  337.3 9.2 %convolution_convert_fusion = bf16[4096,1024]{1,0:T(8,128)(2,1)} fusion(bf16[640,4096]{1,0:T(8,128)(2,1)S(1)} %bitcast.141, bf16[640,1024]{1,0:T(8,128)(2,1)S(1)} %copy-done.24), kind=kOutput, calls=%fused_computation.18 | convolution fusion | flops 5372903424 | bytes 14942208 | tf_op jit(solution)/shard_map/dot_general | solution.py:33
  346.6 0.4 convert_reduce_fusion.1
  347.0 0.8 copy-done.3
  347.9 0.2 convert_reduce_fusion.3
  348.3 0.1 reshape.314
  348.4 0.8 reshape.311
  349.2 0.7 copy.50
  350.0 1.1 reshape.312
  351.1 5.0 %fusion.29 = (f32[1024]{0:T(1024)S(1)}, f32[1024]{0:T(1024)S(1)}, f32[640,1024]{1,0:T(8,128)}) fusion(f32[640]{0:T(1024)} %copy-done.25, bf16[640,1024]{1,0:T(8,128)(2,1)S(1)} %copy-done.3, bf16[1024,1024]{1,0:T(8,128)(2,1)S(1)} %bitcast.118, f32[640,1024]{1,0:T(8,128)} %copy-done.10, f32[640]{0:T(1024)} %copy-done.31), kind=kOutput, calls=%fused_computation.132 | convolution fusion | flops 1345452032 | bytes 8664064 | tf_op jit(solution)/shard_map/dot_general | solution.py:25
  356.3 2.3 fusion.38
  358.7 5.1 %fusion.28 = (f32[1024]{0:T(1024)S(1)}, f32[1024]{0:T(1024)S(1)}, bf16[1024,1024]{1,0:T(8,128)(2,1)}, f32[1024,1024]{1,0:T(8,128)}) fusion(f32[1024]{0:T(1024)S(1)} %bitcast.139, f32[1024,1024]{1,0:T(8,128)S(1)} %fusion.38, bf16[1024,1024]{1,0:T(8,128)(2,1)S(1)} %copy-done.1, bf16[1024,1024]{1,0:T(8,128)(2,1)S(1)} %bitcast.114), kind=kOutput, calls=%fused_computation.131 | convolution fusion | flops 2152724480 | bytes 14692352 | tf_op jit(solution)/shard_map/dot_general | solution.py:25
  364.6 0.1 reshape.310
  364.8 0.7 copy.57
  365.4 120.6 %scatter.1 = (f32[12,256,128]{2,1,0:T(8,128)}, f32[8,128]{1,0:T(8,128)}, bf16[640,1024]{1,0:T(8,128)(2,1)}) custom-call(bf16[4,256,1024]{2,1,0:T(8,128)(2,1)} %bitcast.119, bf16[4,256,1024]{2,1,0:T(8,128)(2,1)} %bitcast.120, bf16[4,256,1024]{2,1,0:T(8,128)(2,1)} %bitcast.121, bf16[4,256,1024]{2,1,0:T(8,128)(2,1)} %bitcast.122, ...), custom_call_target="tpu_custom_call" | custom-call | tf_op jit(solution)/shard_map/scatter/pallas_call | solution.py:451
  486.1 4.9 select_add_fusion
  491.1 0.5 slice_bitcast_fusion.3
  491.7 0.9 copy.53
  492.7 0.6 slice.115
  493.3 0.7 slice_bitcast_fusion.1
  493.9 1.0 fusion.35
  495.0 0.7 reshape.319
  (159 shorter events, 2.3 us)
Async XLA Ops:
  0.6 6.5 %copy-start.22 = (bf16[640,1024]{1,0:T(8,128)(2,1)S(1)}, bf16[640,1024]{1,0:T(8,128)(2,1)}, u32[]{:S(2)}) copy-start(bf16[640,1024]{1,0:T(8,128)(2,1)} %param.18) | copy-start | bytes 3932164
  6.6 0.5 copy-start.39
  7.2 181.3 %copy-start.25 = (f32[640]{0:T(1024)}, f32[640]{0:T(1024)S(1)}, u32[]{:S(2)}) copy-start(f32[640]{0:T(1024)S(1)} %select_reduce_fusion) | copy-start | bytes 7684
  139.3 11.6 %copy-start.46 = (s32[5]{0:T(128)S(1)}, s32[5]{0:T(128)}, u32[]{:S(2)}) copy-start(s32[5]{0:T(128)} %param.19) | copy-start | bytes 64
  151.2 6.5 %copy-start.12 = (bf16[640,1024]{1,0:T(8,128)(2,1)S(1)}, bf16[640,1024]{1,0:T(8,128)(2,1)}, u32[]{:S(2)}) copy-start(bf16[640,1024]{1,0:T(8,128)(2,1)} %fusion.10.h) | copy-start | bytes 3932164
  157.7 3.4 copy-start.16
  157.7 3.4 copy-start.41
  168.1 20.4 %copy-start.19 = (bf16[1,4,256,1024]{3,2,1,0:T(8,128)(2,1)S(1)}, bf16[1,4,256,1024]{3,2,1,0:T(8,128)(2,1)}, u32[]{:S(2)}) copy-start(bf16[1,4,256,1024]{3,2,1,0:T(8,128)(2,1)} %get-tuple-element.128) | copy-start | bytes 6291460
  168.1 20.4 %copy-start.23 = (bf16[640,1024]{1,0:T(8,128)(2,1)S(1)}, bf16[640,1024]{1,0:T(8,128)(2,1)}, u32[]{:S(2)}) copy-start(bf16[640,1024]{1,0:T(8,128)(2,1)} %param.18) | copy-start | bytes 3932164
  168.1 20.4 %copy-start.34 = (f32[1024]{0:T(1024)S(1)}, f32[1024]{0:T(1024)}, u32[]{:S(2)}) copy-start(f32[1024]{0:T(1024)} %param.22) | copy-start | bytes 12292
  168.1 20.4 %copy-start.35 = (f32[1024]{0:T(1024)S(1)}, f32[1024]{0:T(1024)}, u32[]{:S(2)}) copy-start(f32[1024]{0:T(1024)} %param.21) | copy-start | bytes 12292
  168.1 20.4 %copy-start.43 = (f32[1024]{0:T(1024)S(1)}, f32[1024]{0:T(1024)}, u32[]{:S(2)}) copy-start(f32[1024]{0:T(1024)} %param.26) | copy-start | bytes 12292
  188.5 1.9 copy-start.6
  188.5 2.7 slice-start
  188.6 4.8 slice-start.1
  190.4 39.3 %copy-start.8 = (f32[640,1024]{1,0:T(8,128)}, f32[640,1024]{1,0:T(8,128)S(1)}, u32[]{:S(2)}) copy-start(f32[640,1024]{1,0:T(8,128)S(1)} %get-tuple-element.145) | copy-start | bytes 7864324
  190.4 3.0 copy-start.33
  190.4 3.0 copy-start.45
  193.4 36.3 %copy-start.44 = (f32[1024]{0:T(1024)S(1)}, f32[1024]{0:T(1024)}, u32[]{:S(2)}) copy-start(f32[1024]{0:T(1024)} %param.32) | copy-start | bytes 12292
  240.1 1.3 copy-start.14
  240.1 1.3 copy-start.26
  240.5 2.5 copy-start.36
  245.1 1.5 copy-start.11
  266.9 12.2 %copy-start.9 = (f32[640,1024]{1,0:T(8,128)S(1)}, f32[640,1024]{1,0:T(8,128)}, u32[]{:S(2)}) copy-start(f32[640,1024]{1,0:T(8,128)} %copy-done.8) | copy-start | bytes 7864324
  280.0 4.1 copy-start.10
  280.0 2.5 copy-start.20
  280.0 4.1 copy-start.31
  284.1 29.4 %copy-start.13 = (bf16[640,1024]{1,0:T(8,128)(2,1)S(1)}, bf16[640,1024]{1,0:T(8,128)(2,1)}, u32[]{:S(2)}) copy-start(bf16[640,1024]{1,0:T(8,128)(2,1)} %fusion.10.h) | copy-start | bytes 3932164
  313.5 3.2 copy-start.2
  313.5 3.2 copy-start.4
  313.5 33.0 %copy-start = (bf16[1024,1024]{1,0:T(8,128)(2,1)}, bf16[1024,1024]{1,0:T(8,128)(2,1)S(1)}, u32[]{:S(2)}) copy-start(bf16[1024,1024]{1,0:T(8,128)(2,1)S(1)} %get-tuple-element.34) | copy-start | bytes 6291460
  313.6 3.2 copy-start.42
  316.7 10.8 %slice-start.4 = ((s8[5242880]{0:T(1024)(128)(4,1)}), s8[4194304]{0:T(1024)(128)(4,1)S(1)}, s32[]{:S(2)}) async-start(s8[5242880]{0:T(1024)(128)(4,1)} %bitcast.142), calls=%async_computation.4 | async-start | bytes 8388608
  320.5 3.8 copy-start.7
  320.5 7.0 %slice-start.5 = ((s8[5242880]{0:T(1024)(128)(4,1)}), s8[1048576]{0:T(1024)(128)(4,1)S(1)}, s32[]{:S(2)}) async-start(s8[5242880]{0:T(1024)(128)(4,1)} %bitcast.142), calls=%async_computation.5 | async-start | bytes 2097152
  324.3 13.0 %slice-start.2 = ((s8[5242880]{0:T(1024)(128)(4,1)}), s8[1048576]{0:T(1024)(128)(4,1)S(1)}, s32[]{:S(2)}) async-start(s8[5242880]{0:T(1024)(128)(4,1)} %bitcast.140), calls=%async_computation.2 | async-start | bytes 2097152
  327.5 9.8 %copy-start.24 = (bf16[640,1024]{1,0:T(8,128)(2,1)S(1)}, bf16[640,1024]{1,0:T(8,128)(2,1)}, u32[]{:S(2)}) copy-start(bf16[640,1024]{1,0:T(8,128)(2,1)} %get-tuple-element.115) | copy-start | bytes 3932164
  327.5 9.8 %slice-start.3 = ((s8[5242880]{0:T(1024)(128)(4,1)}), s8[4194304]{0:T(1024)(128)(4,1)S(1)}, s32[]{:S(2)}) async-start(s8[5242880]{0:T(1024)(128)(4,1)} %bitcast.140), calls=%async_computation.3 | async-start | bytes 8388608
  346.6 1.3 copy-start.3
  346.6 4.5 copy-start.18
  351.1 5.0 %copy-start.40 = (f32[5]{0:T(128)S(1)}, f32[5]{0:T(128)}, u32[]{:S(2)}) copy-start(f32[5]{0:T(128)} %copy-done.39) | copy-start | bytes 64
  351.1 5.2 %copy-start.5 = (bf16[1024,1024]{1,0:T(8,128)(2,1)S(1)}, bf16[1024,1024]{1,0:T(8,128)(2,1)}, u32[]{:S(2)}) copy-start(bf16[1024,1024]{1,0:T(8,128)(2,1)} %copy-done.4) | copy-start | bytes 6291460
  351.1 5.2 %copy-start.17 = (bf16[1,4,256,1024]{3,2,1,0:T(8,128)(2,1)S(1)}, bf16[1,4,256,1024]{3,2,1,0:T(8,128)(2,1)}, u32[]{:S(2)}) copy-start(bf16[1,4,256,1024]{3,2,1,0:T(8,128)(2,1)} %get-tuple-element.130) | copy-start | bytes 6291460
  356.3 2.4 copy-start.1
  356.3 2.4 copy-start.15
  358.6 5.4 %copy-start.30 = (f32[1024]{0:T(1024)S(1)}, f32[1024]{0:T(1024)}, u32[]{:S(2)}) copy-start(f32[1024]{0:T(1024)} %get-tuple-element.116) | copy-start | bytes 12292
  358.6 5.4 %copy-start.38 = (f32[1024]{0:T(1024)S(1)}, f32[1024]{0:T(1024)}, u32[]{:S(2)}) copy-start(f32[1024]{0:T(1024)} %get-tuple-element.102) | copy-start | bytes 12292
  358.7 5.5 %copy-start.37 = (f32[1024]{0:T(1024)S(1)}, f32[1024]{0:T(1024)}, u32[]{:S(2)}) copy-start(f32[1024]{0:T(1024)} %get-tuple-element.108) | copy-start | bytes 12292
  358.7 5.6 %copy-start.29 = (f32[1024]{0:T(1024)S(1)}, f32[1024]{0:T(1024)}, u32[]{:S(2)}) copy-start(f32[1024]{0:T(1024)} %get-tuple-element.114) | copy-start | bytes 12292
  358.7 5.7 %copy-start.28 = (f32[1024]{0:T(1024)S(1)}, f32[1024]{0:T(1024)}, u32[]{:S(2)}) copy-start(f32[1024]{0:T(1024)} %get-tuple-element.106) | copy-start | bytes 12292
  358.7 5.8 %copy-start.27 = (f32[1024]{0:T(1024)S(1)}, f32[1024]{0:T(1024)}, u32[]{:S(2)}) copy-start(f32[1024]{0:T(1024)} %get-tuple-element.111) | copy-start | bytes 12292
  486.1 5.0 %copy-start.32 = (f32[8,128]{1,0:T(8,128)S(1)}, f32[8,128]{1,0:T(8,128)}, u32[]{:S(2)}) copy-start(f32[8,128]{1,0:T(8,128)} %get-tuple-element.36) | copy-start | bytes 12292
  486.1 5.6 %copy-start.21 = (f32[12,256,128]{2,1,0:T(8,128)S(1)}, f32[12,256,128]{2,1,0:T(8,128)}, u32[]{:S(2)}) copy-start(f32[12,256,128]{2,1,0:T(8,128)} %get-tuple-element.37) | copy-start | bytes 4718596
